TPU v7x, 256 devices: a whole 4x4x8 slice. The times are simulated.
256 devices in a mesh: layer: 8 (over z_hi, core), dict: 32 (over x, y, z_lo).
Axes of the slice: x: 4, y: 4, z: 8 (z_hi: 4, z_lo: 2; z = z_hi * 2 + z_lo), core: 2. Of those that a mesh axis runs over, the one named last changes fastest.
Arguments:
- hidden: bfloat16 [8, 512, 9216], P('layer', None, 'dict'), may hold values from -6 to 6
- row_list: int32 [512], replicated, may hold values from 0 to 511, each once
- w_down: bfloat16 [8, 9216, 2304], P('layer', 'dict'), may hold values from -0.0625 to 0.0625
- w_enc: bfloat16 [8, 2304, 16384], P('layer', None, 'dict'), may hold values from -0.046875 to 0.046875
- b_enc: float32 [16384], P('dict'), may hold values from -3 to 3
- w_dec: float32 [8, 16384, 2304], P('layer', 'dict'), may hold values from -0.046875 to 0.046875
- b_dec: float32 [8, 2304], P('layer'), may hold values from -3 to 3
- alive_mask: int32 [16384], P('dict'), may hold values 0 or 1
Outputs:
- latent: bfloat16 [512, 16384], P('layer', 'dict')
- residual: float32 [8, 512, 2304], P('layer', 'dict')
- adjoint: float32 [512, 16384], P('layer', 'dict')
Inputs may be any that keep to these rules, and one draw needn't show every extreme that they name: `row_list`: a permutation of the 512 buffer rows.
All inputs are finite; a program needn't handle non-finite values. No bound on the sum of `alive_mask` on one device may be relied on, other than what follows from the above.
Results may differ from a plain program's by a relative error of at most 0.0045.
Values may be sent and summed in bfloat16 or wider, within the bound.
No kernel may reach another device: no remote copies, remote signals or barrier semaphores. Data moves between devices by JAX's collectives and lax.ppermute only.
A program may use at most 64 MiB of HBM per device.

v0:
```python
import jax
import jax.numpy as jnp
from jax import lax
from jax.sharding import PartitionSpec as P


F32 = jnp.float32
BF16 = jnp.bfloat16
AXES = ("layer", "dict")


def where_is(i):
    l, d = divmod(i, 32)
    return l >> 1, l & 1, d >> 3, (d >> 1) & 3, d & 1


def number_of(zh, c, x, y, z):
    return (zh * 2 + c) * 32 + x * 8 + y * 2 + z


def swap(value, partner):
    pairs = [(i, number_of(*partner(*where_is(i)))) for i in range(256)]
    return lax.ppermute(value, AXES, pairs)


def swap_far(value, s):
    return swap(value, along_u(gray(s)))


def along_u(d):
    return lambda zh, c, x, y, z: (zh, c, x ^ d, y, z) if c == 0 else (zh, c, x, y ^ d, z)


def along_v(d):
    return lambda zh, c, x, y, z: (zh, c, x, y ^ d, z) if c == 0 else (zh, c, x ^ d, y, z)


def along_z(zh, c, x, y, z):
    return (zh, c, x, y, z ^ 1)


def along_core(zh, c, x, y, z):
    return (zh, c ^ 1, x, y, z)


def along_zh(d):
    return lambda zh, c, x, y, z: (zh ^ d, c, x, y, z)


def gray(s):
    return s ^ (s >> 1)


SLOTS = (1, 2, 3)


def dot(a, b):
    return jnp.dot(a, b, preferred_element_type=F32)


def add(a, b):
    return a + b.astype(F32)


def scatter_sum(part, last):
    sent = [swap_far(part(s).astype(BF16), s) for s in SLOTS]
    total = part(0)
    for got in sent:
        total = add(total, got)
    n = total.shape[0] // 4
    sent = [swap(total[s * n:(s + 1) * n].astype(BF16), along_v(gray(s))) for s in SLOTS]
    total = total[:n]
    for got in sent:
        total = add(total, got)
    n = n // 2
    got = swap(total.astype(last), along_z)
    got = got.astype(F32)
    return total + jnp.concatenate([got[n:], got[:n]], 0)


def gather_rows(two):
    eight = jnp.concatenate([two] + [swap(two, along_v(gray(s))) for s in SLOTS], 0)
    one, three, far = [swap_far(eight, s) for s in SLOTS]
    return [eight, one, three, far]


def turn(a):
    r, n = a.shape
    return a.reshape(4, 4, r // 16, n).transpose(1, 0, 2, 3).reshape(r, n)


def layer_sum(blocks, c, t):
    half = blocks[0].shape[1] // 2
    got = swap(jnp.concatenate([block[:, half:] for block in blocks], 0), along_core)
    mine = jnp.concatenate([block[:, :half] for block in blocks], 0)
    first = jnp.where(c == 0, mine, got)
    second = jnp.where(c == 0, got, mine)
    both = first + turn(second)
    n = both.shape[0] // 4

    def block(d):
        return lax.dynamic_slice_in_dim(both, gray(t ^ d) * n, n, 0)

    sent = [swap(block(gray(s)).astype(BF16), along_zh(gray(s))) for s in SLOTS]
    total = block(0)
    for got in sent:
        total = total + got.astype(F32)
    return total


def per_device(hidden, row_list, w_down, w_enc, b_enc, w_dec, b_dec, alive_mask):
    hidden, w_down, w_enc, w_dec = hidden[0], w_down[0], w_enc[0], w_dec[0]
    rows = hidden.shape[0]
    share = rows // 32
    l, i = lax.axis_index("layer"), lax.axis_index("dict")
    zh, c = l >> 1, l & 1
    x, y, z = i >> 3, (i >> 1) & 3, i & 1
    t = zh ^ x

    p = lax.iota(jnp.int32, rows)
    block = p // share
    du, dv, dz = gray(block >> 3), gray((block >> 1) & 3), block & 1
    dx, dy = jnp.where(c == 0, du, dv), jnp.where(c == 0, dv, du)
    place = (((dx ^ x) * 8) + ((dy ^ y) * 2) + (dz ^ z)) * share + p % share
    ids = jnp.sum(jnp.where(place[:, None] == p[None, :], row_list[None, :], 0), axis=1)
    pick = (ids[:, None] == p[None, :]).astype(BF16)
    chosen = dot(pick, hidden).astype(BF16)
    n = rows // 4
    half = w_enc.shape[1] // 2

    def own_first(w, axis):
        return jnp.concatenate([lax.dynamic_slice_in_dim(w, side * half, half, axis) for side in (c, 1 - c)], axis)

    enc = own_first(w_enc, 1)

    def produced(s):
        return dot(chosen[s * n:(s + 1) * n], w_down)

    acts_two = scatter_sum(produced, F32)
    acts_two = acts_two.astype(BF16)
    dec = w_dec.astype(BF16)
    rest = (w_dec - dec.astype(F32)).astype(BF16)
    dec_high, dec_low = own_first(dec, 0), own_first(rest, 0)
    acts = gather_rows(acts_two)
    first = dot(acts[0], enc)
    preact = layer_sum([first] + [dot(piece, enc) for piece in acts[1:]], c, t)

    alive = alive_mask.astype(F32)
    alive_half = lax.dynamic_slice_in_dim(alive, c * half, half, 0)
    bias_half = lax.dynamic_slice_in_dim(b_enc, c * half, half, 0)
    lat = (jnp.maximum(preact + bias_half, 0.0) * alive_half).astype(BF16)
    side = jnp.concatenate([lat] + [swap(lat, along_zh(gray(s))) for s in SLOTS], 0)
    wide = jnp.concatenate([side, swap(side, along_core)], 1)
    top = c ^ (y >> 1)

    def all_latents(a):
        return jnp.where(c == 0, a, jnp.concatenate([a[..., half:], a[..., :half]], -1))

    latent_own = lax.dynamic_index_in_dim(wide[:n].reshape(2, 2, 2, share, -1), top, 0, keepdims=False)

    def in_place(a):
        a = jnp.where(((y & 1) ^ top) == 0, a, a[::-1])
        a = jnp.where(z == 0, a, a[:, ::-1])
        return a.reshape(4 * share, -1)

    latent_out = in_place(all_latents(latent_own))
    by_x = jnp.concatenate([lax.dynamic_slice_in_dim(wide, gray(t ^ gray(s)) * n, n, 0) for s in range(4)], 0)
    by_u = jnp.where(c == 0, by_x, turn(by_x))

    rebuilt = scatter_sum(lambda s: dot(by_u[s * n:(s + 1) * n], dec_high), BF16)
    residual = acts_two.astype(F32) - (rebuilt + b_dec)
    remainder = gather_rows(residual.astype(BF16))

    def times(piece):
        high, low = [lax.dot_general(piece, w, (((1,), (1,)), ((), ())), preferred_element_type=F32) for w in (dec_high, dec_low)]
        return high + low

    first = times(remainder[0])
    summed = layer_sum([first] + [times(piece) for piece in remainder[1:]], c, t) * -alive_half
    summed = summed.reshape(2, 2, 2, share, half)
    keep = lax.dynamic_index_in_dim(summed, top, 0, keepdims=False)
    give = lax.dynamic_index_in_dim(summed, 1 - top, 0, keepdims=False)
    got = swap(give.reshape(4 * share, half), along_core).reshape(keep.shape)
    adjoint = all_latents(jnp.concatenate([keep, got], -1))
    return latent_out, residual[None, :share], in_place(adjoint)


def solution(mesh):
    return jax.shard_map(
        per_device,
        mesh=mesh,
        in_specs=(
            P("layer", None, "dict"),
            P(),
            P("layer", "dict", None),
            P("layer", None, "dict"),
            P("dict"),
            P("layer", "dict", None),
            P("layer", None),
            P("dict"),
        ),
        out_specs=(P("layer", "dict"), P("layer", "dict", None), P("layer", "dict")),
        check_vma=False,
    )
```

profile of v0, /device:TPU:6, one launch (start us, length us, event | category | flops | bytes accessed | tf_op | source)
XLA Modules:
  0.0 184.8 jit_solution(5541279325279673854)
XLA Ops:
  1.7 1.4 convolution_convert_fusion.6
  5.1 1.5 collective-permute-start.1
  7.1 2.0 %collective-permute-start.2 = (bf16[128,2304]{1,0:T(8,128)(2,1)S(1)}, bf16[128,2304]{1,0:T(8,128)(2,1)S(1)}, u32[]{:S(2)}, u32[]{:S(2)}) collective-permute-start(bf16[128,2304]{1,0:T(8,128)(2,1)S(1)} %convolution_convert_fusion.3), channel_id=1, source_target_pairs={{0,16},{1,17},{2,18},{3,19},{4,20},{5,21},{6,22},{7,23},{8,24},{9,... | collective-permute-start | bytes 1769480 | tf_op jit(solution)/shard_map/ppermute | solution.py:23
  9.0 4.6 %collective-permute-done = bf16[128,2304]{1,0:T(8,128)(2,1)S(1)} collective-permute-done((bf16[128,2304]{1,0:T(8,128)(2,1)S(1)}, bf16[128,2304]{1,0:T(8,128)(2,1)S(1)}, u32[]{:S(2)}, u32[]{:S(2)}) %collective-permute-start) | collective-permute-done | bytes 589856 | tf_op jit(solution)/shard_map/ppermute | solution.py:23
  13.6 9.0 %collective-permute-done.1 = bf16[128,2304]{1,0:T(8,128)(2,1)S(1)} collective-permute-done((bf16[128,2304]{1,0:T(8,128)(2,1)S(1)}, bf16[128,2304]{1,0:T(8,128)(2,1)S(1)}, u32[]{:S(2)}, u32[]{:S(2)}) %collective-permute-start.1) | collective-permute-done | bytes 589856 | tf_op jit(solution)/shard_map/ppermute | solution.py:23
  23.3 1.7 collective-permute-start.3
  24.9 2.9 %collective-permute-start.5 = (bf16[32,2304]{1,0:T(8,128)(2,1)S(1)}, bf16[32,2304]{1,0:T(8,128)(2,1)S(1)}, u32[]{:S(2)}, u32[]{:S(2)}) collective-permute-start(bf16[32,2304]{1,0:T(8,128)(2,1)S(1)} %get-tuple-element.19), channel_id=1, source_target_pairs={{0,4},{1,5},{2,6},{3,7},{4,0},{5,1},{6,2},{7,3},{8,12},{9,13},{10,... | collective-permute-start | bytes 442376 | tf_op jit(solution)/shard_map/ppermute | solution.py:23
  28.5 4.0 %collective-permute-done.5 = bf16[32,2304]{1,0:T(8,128)(2,1)S(1)} collective-permute-done((bf16[32,2304]{1,0:T(8,128)(2,1)S(1)}, bf16[32,2304]{1,0:T(8,128)(2,1)S(1)}, u32[]{:S(2)}, u32[]{:S(2)}) %collective-permute-start.5) | collective-permute-done | bytes 147488 | tf_op jit(solution)/shard_map/ppermute | solution.py:23
  32.5 1.7 collective-permute-done.4
  34.2 2.0 %collective-permute-start.6 = (f32[32,2304]{1,0:T(8,128)S(1)}, f32[32,2304]{1,0:T(8,128)S(1)}, u32[]{:S(2)}, u32[]{:S(2)}) collective-permute-start(f32[32,2304]{1,0:T(8,128)S(1)} %fusion.12), channel_id=1, source_target_pairs={{0,1},{1,0},{2,3},{3,2},{4,5},{5,4},{6,7},{7,6},{8,9},{9,8},{10,11... | collective-permute-start | bytes 884744 | tf_op jit(solution)/shard_map/ppermute | solution.py:23
  36.3 4.8 %collective-permute-done.6 = f32[32,2304]{1,0:T(8,128)S(1)} collective-permute-done((f32[32,2304]{1,0:T(8,128)S(1)}, f32[32,2304]{1,0:T(8,128)S(1)}, u32[]{:S(2)}, u32[]{:S(2)}) %collective-permute-start.6) | collective-permute-done | bytes 294944 | tf_op jit(solution)/shard_map/ppermute | solution.py:23
  42.2 1.7 collective-permute-start.8
  44.7 3.3 %collective-permute-done.9 = bf16[32,2304]{1,0:T(8,128)(2,1)S(1)} collective-permute-done((bf16[32,2304]{1,0:T(8,128)(2,1)S(1)}, bf16[32,2304]{1,0:T(8,128)(2,1)S(1)}, u32[]{:S(2)}, u32[]{:S(2)}) %collective-permute-start.9) | collective-permute-done | bytes 147488 | tf_op jit(solution)/shard_map/ppermute | solution.py:23
  47.9 3.4 %collective-permute-done.8 = bf16[32,2304]{1,0:T(8,128)(2,1)S(1)} collective-permute-done((bf16[32,2304]{1,0:T(8,128)(2,1)S(1)}, bf16[32,2304]{1,0:T(8,128)(2,1)S(1)}, u32[]{:S(2)}, u32[]{:S(2)}) %collective-permute-start.8) | collective-permute-done | bytes 147488 | tf_op jit(solution)/shard_map/ppermute | solution.py:23
  51.4 1.8 dynamic-slice_bitcast_fusion.1
  53.2 1.6 collective-permute-start.11
  54.8 2.0 %collective-permute-start.10 = (bf16[128,2304]{1,0:T(8,128)(2,1)S(1)}, bf16[128,2304]{1,0:T(8,128)(2,1)S(1)}, u32[]{:S(2)}, u32[]{:S(2)}) collective-permute-start(bf16[128,2304]{1,0:T(8,128)(2,1)S(1)} %pad_maximum_fusion.3), channel_id=1, source_target_pairs={{0,8},{1,9},{2,10},{3,11},{4,12},{5,13},{6,14},{7,15},{8,0},{9,1},... | collective-permute-start | bytes 1769480 | tf_op jit(solution)/shard_map/ppermute | solution.py:23
  57.3 5.6 %collective-permute-done.12 = bf16[128,2304]{1,0:T(8,128)(2,1)S(1)} collective-permute-done((bf16[128,2304]{1,0:T(8,128)(2,1)S(1)}, bf16[128,2304]{1,0:T(8,128)(2,1)S(1)}, u32[]{:S(2)}, u32[]{:S(2)}) %collective-permute-start.12) | collective-permute-done | bytes 589856 | tf_op jit(solution)/shard_map/ppermute | solution.py:23
  63.4 5.7 %collective-permute-done.11 = bf16[128,2304]{1,0:T(8,128)(2,1)S(1)} collective-permute-done((bf16[128,2304]{1,0:T(8,128)(2,1)S(1)}, bf16[128,2304]{1,0:T(8,128)(2,1)S(1)}, u32[]{:S(2)}, u32[]{:S(2)}) %collective-permute-start.11) | collective-permute-done | bytes 589856 | tf_op jit(solution)/shard_map/ppermute | solution.py:23
  70.9 1.5 collective-permute-done.13
  72.7 3.4 %collective-permute-start.14 = (bf16[128,256]{1,0:T(8,128)(2,1)S(1)}, bf16[128,256]{1,0:T(8,128)(2,1)S(1)}, u32[]{:S(2)}, u32[]{:S(2)}) collective-permute-start(bf16[128,256]{1,0:T(8,128)(2,1)S(1)} %get-tuple-element.29), channel_id=1, source_target_pairs={{0,64},{1,65},{2,66},{3,67},{4,68},{5,69},{6,70},{7,71},{8,72},{9,... | collective-permute-start | bytes 196616 | tf_op jit(solution)/shard_map/ppermute | solution.py:23
  76.1 5.7 %collective-permute-start.16 = (bf16[128,256]{1,0:T(8,128)(2,1)S(1)}, bf16[128,256]{1,0:T(8,128)(2,1)S(1)}, u32[]{:S(2)}, u32[]{:S(2)}) collective-permute-start(bf16[128,256]{1,0:T(8,128)(2,1)S(1)} %get-tuple-element.30), channel_id=1, source_target_pairs={{0,128},{1,129},{2,130},{3,131},{4,132},{5,133},{6,134},{7,135},{8... | collective-permute-start | bytes 196616 | tf_op jit(solution)/shard_map/ppermute | solution.py:23
  81.8 3.5 %collective-permute-done.16 = bf16[128,256]{1,0:T(8,128)(2,1)S(1)} collective-permute-done((bf16[128,256]{1,0:T(8,128)(2,1)S(1)}, bf16[128,256]{1,0:T(8,128)(2,1)S(1)}, u32[]{:S(2)}, u32[]{:S(2)}) %collective-permute-start.16) | collective-permute-done | bytes 65568 | tf_op jit(solution)/shard_map/ppermute | solution.py:23
  85.3 2.8 %collective-permute-done.15 = bf16[128,256]{1,0:T(8,128)(2,1)S(1)} collective-permute-done((bf16[128,256]{1,0:T(8,128)(2,1)S(1)}, bf16[128,256]{1,0:T(8,128)(2,1)S(1)}, u32[]{:S(2)}, u32[]{:S(2)}) %collective-permute-start.15) | collective-permute-done | bytes 65568 | tf_op jit(solution)/shard_map/ppermute | solution.py:23
  88.2 3.5 %collective-permute-start.19 = (bf16[128,256]{1,0:T(8,128)(2,1)S(1)}, bf16[128,256]{1,0:T(8,128)(2,1)S(1)}, u32[]{:S(2)}, u32[]{:S(2)}) collective-permute-start(bf16[128,256]{1,0:T(8,128)(2,1)S(1)} %multiply_convert_fusion), channel_id=1, source_target_pairs={{0,128},{1,129},{2,130},{3,131},{4,132},{5,133},{6,134},{7,135},{8... | collective-permute-start | bytes 196616 | tf_op jit(solution)/shard_map/ppermute | solution.py:23
  91.6 2.6 %collective-permute-start.18 = (bf16[128,256]{1,0:T(8,128)(2,1)S(1)}, bf16[128,256]{1,0:T(8,128)(2,1)S(1)}, u32[]{:S(2)}, u32[]{:S(2)}) collective-permute-start(bf16[128,256]{1,0:T(8,128)(2,1)S(1)} %multiply_convert_fusion), channel_id=1, source_target_pairs={{0,192},{1,193},{2,194},{3,195},{4,196},{5,197},{6,198},{7,199},{8... | collective-permute-start | bytes 196616 | tf_op jit(solution)/shard_map/ppermute | solution.py:23
  94.7 4.2 %fusion = (bf16[512,2304]{1,0:T(8,128)(2,1)}, bf16[512,2304]{1,0:T(8,128)(2,1)S(1)}) fusion(f32[1,512,2304]{2,1,0:T(8,128)} %param.13), kind=kLoop, calls=%fused_computation.2 | loop fusion | flops 4718592 | bytes 9437184 | tf_op jit(solution)/shard_map/convert_element_type | solution.py:142
  104.3 1.6 collective-permute-start.22
  105.9 1.8 collective-permute-start.21
  107.8 8.0 %collective-permute-done.23 = bf16[128,2304]{1,0:T(8,128)(2,1)S(1)} collective-permute-done((bf16[128,2304]{1,0:T(8,128)(2,1)S(1)}, bf16[128,2304]{1,0:T(8,128)(2,1)S(1)}, u32[]{:S(2)}, u32[]{:S(2)}) %collective-permute-start.23) | collective-permute-done | bytes 589856 | tf_op jit(solution)/shard_map/ppermute | solution.py:23
  115.8 6.0 %collective-permute-done.22 = bf16[128,2304]{1,0:T(8,128)(2,1)S(1)} collective-permute-done((bf16[128,2304]{1,0:T(8,128)(2,1)S(1)}, bf16[128,2304]{1,0:T(8,128)(2,1)S(1)}, u32[]{:S(2)}, u32[]{:S(2)}) %collective-permute-start.22) | collective-permute-done | bytes 589856 | tf_op jit(solution)/shard_map/ppermute | solution.py:23
  122.5 2.2 %collective-permute-start.26 = (bf16[32,2304]{1,0:T(8,128)(2,1)S(1)}, bf16[32,2304]{1,0:T(8,128)(2,1)S(1)}, u32[]{:S(2)}, u32[]{:S(2)}) collective-permute-start(bf16[32,2304]{1,0:T(8,128)(2,1)S(1)} %get-tuple-element.16), channel_id=1, source_target_pairs={{0,4},{1,5},{2,6},{3,7},{4,0},{5,1},{6,2},{7,3},{8,12},{9,13},{10,... | collective-permute-start | bytes 442376 | tf_op jit(solution)/shard_map/ppermute | solution.py:23
  124.7 2.5 %collective-permute-start.25 = (bf16[32,2304]{1,0:T(8,128)(2,1)S(1)}, bf16[32,2304]{1,0:T(8,128)(2,1)S(1)}, u32[]{:S(2)}, u32[]{:S(2)}) collective-permute-start(bf16[32,2304]{1,0:T(8,128)(2,1)S(1)} %get-tuple-element.17), channel_id=1, source_target_pairs={{0,6},{1,7},{2,4},{3,5},{4,2},{5,3},{6,0},{7,1},{8,14},{9,15},{10,... | collective-permute-start | bytes 442376 | tf_op jit(solution)/shard_map/ppermute | solution.py:23
  127.6 1.8 collective-permute-done.26
  129.4 1.7 collective-permute-done.25
  132.6 3.7 %collective-permute-done.27 = bf16[32,2304]{1,0:T(8,128)(2,1)S(1)} collective-permute-done((bf16[32,2304]{1,0:T(8,128)(2,1)S(1)}, bf16[32,2304]{1,0:T(8,128)(2,1)S(1)}, u32[]{:S(2)}, u32[]{:S(2)}) %collective-permute-start.27) | collective-permute-done | bytes 147488 | tf_op jit(solution)/shard_map/ppermute | solution.py:23
  137.5 1.9 %collective-permute-start.30 = (bf16[32,2304]{1,0:T(8,128)(2,1)S(1)}, bf16[32,2304]{1,0:T(8,128)(2,1)S(1)}, u32[]{:S(2)}, u32[]{:S(2)}) collective-permute-start(bf16[32,2304]{1,0:T(8,128)(2,1)S(1)} %get-tuple-element.7), channel_id=1, source_target_pairs={{0,4},{1,5},{2,6},{3,7},{4,0},{5,1},{6,2},{7,3},{8,12},{9,13},{10,... | collective-permute-start | bytes 442376 | tf_op jit(solution)/shard_map/ppermute | solution.py:23
  141.0 3.3 %constant_dynamic-slice_fusion.1 = (bf16[256,2304]{1,0:T(8,128)(2,1)}, bf16[256,2304]{1,0:T(8,128)(2,1)}) fusion(bf16[512,2304]{1,0:T(8,128)(2,1)} %get-tuple-element.5, s32[]{:T(128)S(6)} %select_n.165, s32[]{:T(128)S(6)} %select_n.166), kind=kLoop, calls=%fused_computation.83 | loop fusion | bytes 4718600 | tf_op jit(solution)/shard_map/dynamic_slice | solution.py:132
  144.3 1.4 collective-permute-done.29
  146.9 1.9 %collective-permute-start.33 = (bf16[128,2304]{1,0:T(8,128)(2,1)S(1)}, bf16[128,2304]{1,0:T(8,128)(2,1)S(1)}, u32[]{:S(2)}, u32[]{:S(2)}) collective-permute-start(bf16[128,2304]{1,0:T(8,128)(2,1)S(1)} %pad_maximum_fusion.4), channel_id=1, source_target_pairs={{0,16},{1,17},{2,18},{3,19},{4,20},{5,21},{6,22},{7,23},{8,24},{9,... | collective-permute-start | bytes 1769480 | tf_op jit(solution)/shard_map/ppermute | solution.py:23
  148.8 2.8 %collective-permute-start.32 = (bf16[128,2304]{1,0:T(8,128)(2,1)S(1)}, bf16[128,2304]{1,0:T(8,128)(2,1)S(1)}, u32[]{:S(2)}, u32[]{:S(2)}) collective-permute-start(bf16[128,2304]{1,0:T(8,128)(2,1)S(1)} %pad_maximum_fusion.4), channel_id=1, source_target_pairs={{0,24},{1,25},{2,26},{3,27},{4,28},{5,29},{6,30},{7,31},{8,16},{9,... | collective-permute-start | bytes 1769480 | tf_op jit(solution)/shard_map/ppermute | solution.py:23
  151.6 2.6 %fusion.51 = f32[128,512]{1,0:T(8,128)S(1)} fusion(bf16[256,2304]{1,0:T(8,128)(2,1)} %get-tuple-element.10, bf16[256,2304]{1,0:T(8,128)(2,1)} %get-tuple-element.9, bf16[32,2304]{1,0:T(8,128)(2,1)S(1)} %collective-permute-done.30, bf16[32,2304]{1,0:T(8,128)(2,1)S(1)} %collective-permute-done.29, bf16[32,2304]{1,0:T(8,128)(2,1)S(1)} %collective-permute-done.28, ...), kind=kOutput, calls=%fused_computation.116 | convolution fusion | flops 309067776 | bytes 3211264 | tf_op jit(solution)/shard_map/dot_general | solution.py:175
  155.2 1.6 collective-permute-done.31
  158.6 4.5 %collective-permute-done.33 = bf16[128,2304]{1,0:T(8,128)(2,1)S(1)} collective-permute-done((bf16[128,2304]{1,0:T(8,128)(2,1)S(1)}, bf16[128,2304]{1,0:T(8,128)(2,1)S(1)}, u32[]{:S(2)}, u32[]{:S(2)}) %collective-permute-start.33) | collective-permute-done | bytes 589856 | tf_op jit(solution)/shard_map/ppermute | solution.py:23
  168.3 1.8 collective-permute-done.34
  171.8 3.9 %collective-permute-start.37 = (bf16[128,256]{1,0:T(8,128)(2,1)S(1)}, bf16[128,256]{1,0:T(8,128)(2,1)S(1)}, u32[]{:S(2)}, u32[]{:S(2)}) collective-permute-start(bf16[128,256]{1,0:T(8,128)(2,1)S(1)} %get-tuple-element.22), channel_id=1, source_target_pairs={{0,128},{1,129},{2,130},{3,131},{4,132},{5,133},{6,134},{7,135},{8... | collective-permute-start | bytes 196616 | tf_op jit(solution)/shard_map/ppermute | solution.py:23
  177.6 2.4 %collective-permute-done.37 = bf16[128,256]{1,0:T(8,128)(2,1)S(1)} collective-permute-done((bf16[128,256]{1,0:T(8,128)(2,1)S(1)}, bf16[128,256]{1,0:T(8,128)(2,1)S(1)}, u32[]{:S(2)}, u32[]{:S(2)}) %collective-permute-start.37) | collective-permute-done | bytes 65568 | tf_op jit(solution)/shard_map/ppermute | solution.py:23
  180.0 2.7 %collective-permute-done.36 = bf16[128,256]{1,0:T(8,128)(2,1)S(1)} collective-permute-done((bf16[128,256]{1,0:T(8,128)(2,1)S(1)}, bf16[128,256]{1,0:T(8,128)(2,1)S(1)}, u32[]{:S(2)}, u32[]{:S(2)}) %collective-permute-start.36) | collective-permute-done | bytes 65568 | tf_op jit(solution)/shard_map/ppermute | solution.py:23
  (125 shorter events, 35.7 us)
Async XLA Ops:
  0.6 2.5 %copy-start = (bf16[1,288,2304]{2,1,0:T(8,128)(2,1)S(1)}, bf16[1,288,2304]{2,1,0:T(8,128)(2,1)}, u32[]{:S(2)}) copy-start(bf16[1,288,2304]{2,1,0:T(8,128)(2,1)} %param.10) | copy-start | bytes 3981316
  3.7 10.0 %collective-permute-start = (bf16[128,2304]{1,0:T(8,128)(2,1)S(1)}, bf16[128,2304]{1,0:T(8,128)(2,1)S(1)}, u32[]{:S(2)}, u32[]{:S(2)}) collective-permute-start(bf16[128,2304]{1,0:T(8,128)(2,1)S(1)} %convolution_convert_fusion.5), channel_id=1, source_target_pairs={{0,8},{1,9},{2,10},{3,11},{4,12},{5,13},{6,14},{7,15},{8,0},{9,1},... | collective-permute-start | bytes 1769480 | tf_op jit(solution)/shard_map/ppermute | solution.py:23
  5.1 17.5 %collective-permute-start.1 = (bf16[128,2304]{1,0:T(8,128)(2,1)S(1)}, bf16[128,2304]{1,0:T(8,128)(2,1)S(1)}, u32[]{:S(2)}, u32[]{:S(2)}) collective-permute-start(bf16[128,2304]{1,0:T(8,128)(2,1)S(1)} %convolution_convert_fusion.4), channel_id=1, source_target_pairs={{0,24},{1,25},{2,26},{3,27},{4,28},{5,29},{6,30},{7,31},{8,16},{9,... | collective-permute-start | bytes 1769480 | tf_op jit(solution)/shard_map/ppermute | solution.py:23
  7.1 15.5 %collective-permute-start.2 = (bf16[128,2304]{1,0:T(8,128)(2,1)S(1)}, bf16[128,2304]{1,0:T(8,128)(2,1)S(1)}, u32[]{:S(2)}, u32[]{:S(2)}) collective-permute-start(bf16[128,2304]{1,0:T(8,128)(2,1)S(1)} %convolution_convert_fusion.3), channel_id=1, source_target_pairs={{0,16},{1,17},{2,18},{3,19},{4,20},{5,21},{6,22},{7,23},{8,24},{9,... | collective-permute-start | bytes 1769480 | tf_op jit(solution)/shard_map/ppermute | solution.py:23
  23.3 5.2 %collective-permute-start.3 = (bf16[32,2304]{1,0:T(8,128)(2,1)S(1)}, bf16[32,2304]{1,0:T(8,128)(2,1)S(1)}, u32[]{:S(2)}, u32[]{:S(2)}) collective-permute-start(bf16[32,2304]{1,0:T(8,128)(2,1)S(1)} %get-tuple-element.18), channel_id=1, source_target_pairs={{0,2},{1,3},{2,0},{3,1},{4,6},{5,7},{6,4},{7,5},{8,10},{9,11},{10,... | collective-permute-start | bytes 442376 | tf_op jit(solution)/shard_map/ppermute | solution.py:23
  24.9 7.6 %collective-permute-start.5 = (bf16[32,2304]{1,0:T(8,128)(2,1)S(1)}, bf16[32,2304]{1,0:T(8,128)(2,1)S(1)}, u32[]{:S(2)}, u32[]{:S(2)}) collective-permute-start(bf16[32,2304]{1,0:T(8,128)(2,1)S(1)} %get-tuple-element.19), channel_id=1, source_target_pairs={{0,4},{1,5},{2,6},{3,7},{4,0},{5,1},{6,2},{7,3},{8,12},{9,13},{10,... | collective-permute-start | bytes 442376 | tf_op jit(solution)/shard_map/ppermute | solution.py:23
  27.8 6.4 %collective-permute-start.4 = (bf16[32,2304]{1,0:T(8,128)(2,1)S(1)}, bf16[32,2304]{1,0:T(8,128)(2,1)S(1)}, u32[]{:S(2)}, u32[]{:S(2)}) collective-permute-start(bf16[32,2304]{1,0:T(8,128)(2,1)S(1)} %get-tuple-element.20), channel_id=1, source_target_pairs={{0,6},{1,7},{2,4},{3,5},{4,2},{5,3},{6,0},{7,1},{8,14},{9,15},{10,... | collective-permute-start | bytes 442376 | tf_op jit(solution)/shard_map/ppermute | solution.py:23
  34.2 6.8 %collective-permute-start.6 = (f32[32,2304]{1,0:T(8,128)S(1)}, f32[32,2304]{1,0:T(8,128)S(1)}, u32[]{:S(2)}, u32[]{:S(2)}) collective-permute-start(f32[32,2304]{1,0:T(8,128)S(1)} %fusion.12), channel_id=1, source_target_pairs={{0,1},{1,0},{2,3},{3,2},{4,5},{5,4},{6,7},{7,6},{8,9},{9,8},{10,11... | collective-permute-start | bytes 884744 | tf_op jit(solution)/shard_map/ppermute | solution.py:23
  41.1 6.8 %collective-permute-start.9 = (bf16[32,2304]{1,0:T(8,128)(2,1)S(1)}, bf16[32,2304]{1,0:T(8,128)(2,1)S(1)}, u32[]{:S(2)}, u32[]{:S(2)}) collective-permute-start(bf16[32,2304]{1,0:T(8,128)(2,1)S(1)} %fusion.13), channel_id=1, source_target_pairs={{0,4},{1,5},{2,6},{3,7},{4,0},{5,1},{6,2},{7,3},{8,12},{9,13},{10,... | collective-permute-start | bytes 442376 | tf_op jit(solution)/shard_map/ppermute | solution.py:23
  42.2 9.1 %collective-permute-start.8 = (bf16[32,2304]{1,0:T(8,128)(2,1)S(1)}, bf16[32,2304]{1,0:T(8,128)(2,1)S(1)}, u32[]{:S(2)}, u32[]{:S(2)}) collective-permute-start(bf16[32,2304]{1,0:T(8,128)(2,1)S(1)} %fusion.13), channel_id=1, source_target_pairs={{0,6},{1,7},{2,4},{3,5},{4,2},{5,3},{6,0},{7,1},{8,14},{9,15},{10,... | collective-permute-start | bytes 442376 | tf_op jit(solution)/shard_map/ppermute | solution.py:23
  43.9 7.4 %collective-permute-start.7 = (bf16[32,2304]{1,0:T(8,128)(2,1)S(1)}, bf16[32,2304]{1,0:T(8,128)(2,1)S(1)}, u32[]{:S(2)}, u32[]{:S(2)}) collective-permute-start(bf16[32,2304]{1,0:T(8,128)(2,1)S(1)} %fusion.13), channel_id=1, source_target_pairs={{0,2},{1,3},{2,0},{3,1},{4,6},{5,7},{6,4},{7,5},{8,10},{9,11},{10,... | collective-permute-start | bytes 442376 | tf_op jit(solution)/shard_map/ppermute | solution.py:23
  51.3 11.6 %collective-permute-start.12 = (bf16[128,2304]{1,0:T(8,128)(2,1)S(1)}, bf16[128,2304]{1,0:T(8,128)(2,1)S(1)}, u32[]{:S(2)}, u32[]{:S(2)}) collective-permute-start(bf16[128,2304]{1,0:T(8,128)(2,1)S(1)} %pad_maximum_fusion.3), channel_id=1, source_target_pairs={{0,16},{1,17},{2,18},{3,19},{4,20},{5,21},{6,22},{7,23},{8,24},{9,... | collective-permute-start | bytes 1769480 | tf_op jit(solution)/shard_map/ppermute | solution.py:23
  53.2 15.9 %collective-permute-start.11 = (bf16[128,2304]{1,0:T(8,128)(2,1)S(1)}, bf16[128,2304]{1,0:T(8,128)(2,1)S(1)}, u32[]{:S(2)}, u32[]{:S(2)}) collective-permute-start(bf16[128,2304]{1,0:T(8,128)(2,1)S(1)} %pad_maximum_fusion.3), channel_id=1, source_target_pairs={{0,24},{1,25},{2,26},{3,27},{4,28},{5,29},{6,30},{7,31},{8,16},{9,... | collective-permute-start | bytes 1769480 | tf_op jit(solution)/shard_map/ppermute | solution.py:23
  54.8 14.8 %collective-permute-start.10 = (bf16[128,2304]{1,0:T(8,128)(2,1)S(1)}, bf16[128,2304]{1,0:T(8,128)(2,1)S(1)}, u32[]{:S(2)}, u32[]{:S(2)}) collective-permute-start(bf16[128,2304]{1,0:T(8,128)(2,1)S(1)} %pad_maximum_fusion.3), channel_id=1, source_target_pairs={{0,8},{1,9},{2,10},{3,11},{4,12},{5,13},{6,14},{7,15},{8,0},{9,1},... | collective-permute-start | bytes 1769480 | tf_op jit(solution)/shard_map/ppermute | solution.py:23
  70.1 0.7 copy-start.8
  70.2 0.7 copy-start.7
  70.2 2.2 %collective-permute-start.13 = (f32[512,256]{1,0:T(8,128)S(1)}, f32[512,256]{1,0:T(8,128)S(1)}, u32[]{:S(2)}, u32[]{:S(2)}) collective-permute-start(f32[512,256]{1,0:T(8,128)S(1)} %pad_maximum_fusion.6), channel_id=1, source_target_pairs={{0,32},{1,33},{2,34},{3,35},{4,36},{5,37},{6,38},{7,39},{8,40},{9,... | collective-permute-start | bytes 1572872 | tf_op jit(solution)/shard_map/ppermute | solution.py:23
  72.7 9.1 %collective-permute-start.14 = (bf16[128,256]{1,0:T(8,128)(2,1)S(1)}, bf16[128,256]{1,0:T(8,128)(2,1)S(1)}, u32[]{:S(2)}, u32[]{:S(2)}) collective-permute-start(bf16[128,256]{1,0:T(8,128)(2,1)S(1)} %get-tuple-element.29), channel_id=1, source_target_pairs={{0,64},{1,65},{2,66},{3,67},{4,68},{5,69},{6,70},{7,71},{8,72},{9,... | collective-permute-start | bytes 196616 | tf_op jit(solution)/shard_map/ppermute | solution.py:23
  76.1 9.3 %collective-permute-start.16 = (bf16[128,256]{1,0:T(8,128)(2,1)S(1)}, bf16[128,256]{1,0:T(8,128)(2,1)S(1)}, u32[]{:S(2)}, u32[]{:S(2)}) collective-permute-start(bf16[128,256]{1,0:T(8,128)(2,1)S(1)} %get-tuple-element.30), channel_id=1, source_target_pairs={{0,128},{1,129},{2,130},{3,131},{4,132},{5,133},{6,134},{7,135},{8... | collective-permute-start | bytes 196616 | tf_op jit(solution)/shard_map/ppermute | solution.py:23
  81.7 6.4 %collective-permute-start.15 = (bf16[128,256]{1,0:T(8,128)(2,1)S(1)}, bf16[128,256]{1,0:T(8,128)(2,1)S(1)}, u32[]{:S(2)}, u32[]{:S(2)}) collective-permute-start(bf16[128,256]{1,0:T(8,128)(2,1)S(1)} %get-tuple-element.31), channel_id=1, source_target_pairs={{0,192},{1,193},{2,194},{3,195},{4,196},{5,197},{6,198},{7,199},{8... | collective-permute-start | bytes 196616 | tf_op jit(solution)/shard_map/ppermute | solution.py:23
  88.2 10.8 %collective-permute-start.19 = (bf16[128,256]{1,0:T(8,128)(2,1)S(1)}, bf16[128,256]{1,0:T(8,128)(2,1)S(1)}, u32[]{:S(2)}, u32[]{:S(2)}) collective-permute-start(bf16[128,256]{1,0:T(8,128)(2,1)S(1)} %multiply_convert_fusion), channel_id=1, source_target_pairs={{0,128},{1,129},{2,130},{3,131},{4,132},{5,133},{6,134},{7,135},{8... | collective-permute-start | bytes 196616 | tf_op jit(solution)/shard_map/ppermute | solution.py:23
  91.6 7.3 %collective-permute-start.18 = (bf16[128,256]{1,0:T(8,128)(2,1)S(1)}, bf16[128,256]{1,0:T(8,128)(2,1)S(1)}, u32[]{:S(2)}, u32[]{:S(2)}) collective-permute-start(bf16[128,256]{1,0:T(8,128)(2,1)S(1)} %multiply_convert_fusion), channel_id=1, source_target_pairs={{0,192},{1,193},{2,194},{3,195},{4,196},{5,197},{6,198},{7,199},{8... | collective-permute-start | bytes 196616 | tf_op jit(solution)/shard_map/ppermute | solution.py:23
  94.2 5.8 %collective-permute-start.17 = (bf16[128,256]{1,0:T(8,128)(2,1)S(1)}, bf16[128,256]{1,0:T(8,128)(2,1)S(1)}, u32[]{:S(2)}, u32[]{:S(2)}) collective-permute-start(bf16[128,256]{1,0:T(8,128)(2,1)S(1)} %multiply_convert_fusion), channel_id=1, source_target_pairs={{0,64},{1,65},{2,66},{3,67},{4,68},{5,69},{6,70},{7,71},{8,72},{9,... | collective-permute-start | bytes 196616 | tf_op jit(solution)/shard_map/ppermute | solution.py:23
  100.1 1.6 collective-permute-start.20
  100.3 21.5 %copy-start.1 = (bf16[256,2304]{1,0:T(8,128)(2,1)}, bf16[256,2304]{1,0:T(8,128)(2,1)S(1)}, u32[]{:S(2)}) copy-start(bf16[256,2304]{1,0:T(8,128)(2,1)S(1)} %get-tuple-element.12) | copy-start | bytes 3538948
  104.2 11.6 %collective-permute-start.23 = (bf16[128,2304]{1,0:T(8,128)(2,1)S(1)}, bf16[128,2304]{1,0:T(8,128)(2,1)S(1)}, u32[]{:S(2)}, u32[]{:S(2)}) collective-permute-start(bf16[128,2304]{1,0:T(8,128)(2,1)S(1)} %convolution_convert_fusion), channel_id=1, source_target_pairs={{0,16},{1,17},{2,18},{3,19},{4,20},{5,21},{6,22},{7,23},{8,24},{9,... | collective-permute-start | bytes 1769480 | tf_op jit(solution)/shard_map/ppermute | solution.py:23
  104.3 17.5 %collective-permute-start.22 = (bf16[128,2304]{1,0:T(8,128)(2,1)S(1)}, bf16[128,2304]{1,0:T(8,128)(2,1)S(1)}, u32[]{:S(2)}, u32[]{:S(2)}) collective-permute-start(bf16[128,2304]{1,0:T(8,128)(2,1)S(1)} %convolution_convert_fusion.1), channel_id=1, source_target_pairs={{0,24},{1,25},{2,26},{3,27},{4,28},{5,29},{6,30},{7,31},{8,16},{9,... | collective-permute-start | bytes 1769480 | tf_op jit(solution)/shard_map/ppermute | solution.py:23
  105.9 15.9 %collective-permute-start.21 = (bf16[128,2304]{1,0:T(8,128)(2,1)S(1)}, bf16[128,2304]{1,0:T(8,128)(2,1)S(1)}, u32[]{:S(2)}, u32[]{:S(2)}) collective-permute-start(bf16[128,2304]{1,0:T(8,128)(2,1)S(1)} %convolution_convert_fusion.2), channel_id=1, source_target_pairs={{0,8},{1,9},{2,10},{3,11},{4,12},{5,13},{6,14},{7,15},{8,0},{9,1},... | collective-permute-start | bytes 1769480 | tf_op jit(solution)/shard_map/ppermute | solution.py:23
  122.3 8.7 %copy-start.6 = (f32[128,2304]{1,0:T(8,128)}, f32[128,2304]{1,0:T(8,128)S(1)}, u32[]{:S(2)}) copy-start(f32[128,2304]{1,0:T(8,128)S(1)} %get-tuple-element.59) | copy-start | bytes 3538948
  122.4 5.2 %collective-permute-start.24 = (bf16[32,2304]{1,0:T(8,128)(2,1)S(1)}, bf16[32,2304]{1,0:T(8,128)(2,1)S(1)}, u32[]{:S(2)}, u32[]{:S(2)}) collective-permute-start(bf16[32,2304]{1,0:T(8,128)(2,1)S(1)} %get-tuple-element.15), channel_id=1, source_target_pairs={{0,2},{1,3},{2,0},{3,1},{4,6},{5,7},{6,4},{7,5},{8,10},{9,11},{10,... | collective-permute-start | bytes 442376 | tf_op jit(solution)/shard_map/ppermute | solution.py:23
  122.5 6.9 %collective-permute-start.26 = (bf16[32,2304]{1,0:T(8,128)(2,1)S(1)}, bf16[32,2304]{1,0:T(8,128)(2,1)S(1)}, u32[]{:S(2)}, u32[]{:S(2)}) collective-permute-start(bf16[32,2304]{1,0:T(8,128)(2,1)S(1)} %get-tuple-element.16), channel_id=1, source_target_pairs={{0,4},{1,5},{2,6},{3,7},{4,0},{5,1},{6,2},{7,3},{8,12},{9,13},{10,... | collective-permute-start | bytes 442376 | tf_op jit(solution)/shard_map/ppermute | solution.py:23
  124.7 6.4 %collective-permute-start.25 = (bf16[32,2304]{1,0:T(8,128)(2,1)S(1)}, bf16[32,2304]{1,0:T(8,128)(2,1)S(1)}, u32[]{:S(2)}, u32[]{:S(2)}) collective-permute-start(bf16[32,2304]{1,0:T(8,128)(2,1)S(1)} %get-tuple-element.17), channel_id=1, source_target_pairs={{0,6},{1,7},{2,4},{3,5},{4,2},{5,3},{6,0},{7,1},{8,14},{9,15},{10,... | collective-permute-start | bytes 442376 | tf_op jit(solution)/shard_map/ppermute | solution.py:23
  131.1 5.2 %collective-permute-start.27 = (bf16[32,2304]{1,0:T(8,128)(2,1)S(1)}, bf16[32,2304]{1,0:T(8,128)(2,1)S(1)}, u32[]{:S(2)}, u32[]{:S(2)}) collective-permute-start(bf16[32,2304]{1,0:T(8,128)(2,1)S(1)} %fusion.36), channel_id=1, source_target_pairs={{0,1},{1,0},{2,3},{3,2},{4,5},{5,4},{6,7},{7,6},{8,9},{9,8},{10,11... | collective-permute-start | bytes 442376 | tf_op jit(solution)/shard_map/ppermute | solution.py:23
  137.5 6.9 %collective-permute-start.30 = (bf16[32,2304]{1,0:T(8,128)(2,1)S(1)}, bf16[32,2304]{1,0:T(8,128)(2,1)S(1)}, u32[]{:S(2)}, u32[]{:S(2)}) collective-permute-start(bf16[32,2304]{1,0:T(8,128)(2,1)S(1)} %get-tuple-element.7), channel_id=1, source_target_pairs={{0,4},{1,5},{2,6},{3,7},{4,0},{5,1},{6,2},{7,3},{8,12},{9,13},{10,... | collective-permute-start | bytes 442376 | tf_op jit(solution)/shard_map/ppermute | solution.py:23
  139.3 6.4 %collective-permute-start.29 = (bf16[32,2304]{1,0:T(8,128)(2,1)S(1)}, bf16[32,2304]{1,0:T(8,128)(2,1)S(1)}, u32[]{:S(2)}, u32[]{:S(2)}) collective-permute-start(bf16[32,2304]{1,0:T(8,128)(2,1)S(1)} %get-tuple-element.7), channel_id=1, source_target_pairs={{0,6},{1,7},{2,4},{3,5},{4,2},{5,3},{6,0},{7,1},{8,14},{9,15},{10,... | collective-permute-start | bytes 442376 | tf_op jit(solution)/shard_map/ppermute | solution.py:23
  140.4 6.4 %collective-permute-start.28 = (bf16[32,2304]{1,0:T(8,128)(2,1)S(1)}, bf16[32,2304]{1,0:T(8,128)(2,1)S(1)}, u32[]{:S(2)}, u32[]{:S(2)}) collective-permute-start(bf16[32,2304]{1,0:T(8,128)(2,1)S(1)} %get-tuple-element.7), channel_id=1, source_target_pairs={{0,2},{1,3},{2,0},{3,1},{4,6},{5,7},{6,4},{7,5},{8,10},{9,11},{10,... | collective-permute-start | bytes 442376 | tf_op jit(solution)/shard_map/ppermute | solution.py:23
  141.0 3.3 %copy-start.5 = (bf16[128,512]{1,0:T(8,128)(2,1)S(1)}, bf16[128,512]{1,0:T(8,128)(2,1)}, u32[]{:S(2)}) copy-start(bf16[128,512]{1,0:T(8,128)(2,1)} %get-tuple-element.28) | copy-start | bytes 393220
  146.8 10.0 %collective-permute-start.31 = (bf16[128,2304]{1,0:T(8,128)(2,1)S(1)}, bf16[128,2304]{1,0:T(8,128)(2,1)S(1)}, u32[]{:S(2)}, u32[]{:S(2)}) collective-permute-start(bf16[128,2304]{1,0:T(8,128)(2,1)S(1)} %pad_maximum_fusion.4), channel_id=1, source_target_pairs={{0,8},{1,9},{2,10},{3,11},{4,12},{5,13},{6,14},{7,15},{8,0},{9,1},... | collective-permute-start | bytes 1769480 | tf_op jit(solution)/shard_map/ppermute | solution.py:23
  146.9 16.2 %collective-permute-start.33 = (bf16[128,2304]{1,0:T(8,128)(2,1)S(1)}, bf16[128,2304]{1,0:T(8,128)(2,1)S(1)}, u32[]{:S(2)}, u32[]{:S(2)}) collective-permute-start(bf16[128,2304]{1,0:T(8,128)(2,1)S(1)} %pad_maximum_fusion.4), channel_id=1, source_target_pairs={{0,16},{1,17},{2,18},{3,19},{4,20},{5,21},{6,22},{7,23},{8,24},{9,... | collective-permute-start | bytes 1769480 | tf_op jit(solution)/shard_map/ppermute | solution.py:23
  148.8 17.4 %collective-permute-start.32 = (bf16[128,2304]{1,0:T(8,128)(2,1)S(1)}, bf16[128,2304]{1,0:T(8,128)(2,1)S(1)}, u32[]{:S(2)}, u32[]{:S(2)}) collective-permute-start(bf16[128,2304]{1,0:T(8,128)(2,1)S(1)} %pad_maximum_fusion.4), channel_id=1, source_target_pairs={{0,24},{1,25},{2,26},{3,27},{4,28},{5,29},{6,30},{7,31},{8,16},{9,... | collective-permute-start | bytes 1769480 | tf_op jit(solution)/shard_map/ppermute | solution.py:23
  151.6 2.6 %copy-start.2 = (bf16[256,2304]{1,0:T(8,128)(2,1)S(1)}, bf16[256,2304]{1,0:T(8,128)(2,1)}, u32[]{:S(2)}) copy-start(bf16[256,2304]{1,0:T(8,128)(2,1)} %copy-done.1) | copy-start | bytes 3538948
  154.2 2.6 %copy-start.3 = (bf16[256,2304]{1,0:T(8,128)(2,1)S(1)}, bf16[256,2304]{1,0:T(8,128)(2,1)}, u32[]{:S(2)}) copy-start(bf16[256,2304]{1,0:T(8,128)(2,1)} %get-tuple-element.9) | copy-start | bytes 3538948
  154.2 2.6 %copy-start.4 = (bf16[256,2304]{1,0:T(8,128)(2,1)S(1)}, bf16[256,2304]{1,0:T(8,128)(2,1)}, u32[]{:S(2)}) copy-start(bf16[256,2304]{1,0:T(8,128)(2,1)} %get-tuple-element.10) | copy-start | bytes 3538948
  168.1 2.0 %collective-permute-start.34 = (f32[512,256]{1,0:T(8,128)S(1)}, f32[512,256]{1,0:T(8,128)S(1)}, u32[]{:S(2)}, u32[]{:S(2)}) collective-permute-start(f32[512,256]{1,0:T(8,128)S(1)} %pad_maximum_fusion.10), channel_id=1, source_target_pairs={{0,32},{1,33},{2,34},{3,35},{4,36},{5,37},{6,38},{7,39},{8,40},{9,... | collective-permute-start | bytes 1572872 | tf_op jit(solution)/shard_map/ppermute | solution.py:23
  170.3 7.2 %collective-permute-start.35 = (bf16[128,256]{1,0:T(8,128)(2,1)S(1)}, bf16[128,256]{1,0:T(8,128)(2,1)S(1)}, u32[]{:S(2)}, u32[]{:S(2)}) collective-permute-start(bf16[128,256]{1,0:T(8,128)(2,1)S(1)} %get-tuple-element.21), channel_id=1, source_target_pairs={{0,64},{1,65},{2,66},{3,67},{4,68},{5,69},{6,70},{7,71},{8,72},{9,... | collective-permute-start | bytes 196616 | tf_op jit(solution)/shard_map/ppermute | solution.py:23
  171.8 8.3 %collective-permute-start.37 = (bf16[128,256]{1,0:T(8,128)(2,1)S(1)}, bf16[128,256]{1,0:T(8,128)(2,1)S(1)}, u32[]{:S(2)}, u32[]{:S(2)}) collective-permute-start(bf16[128,256]{1,0:T(8,128)(2,1)S(1)} %get-tuple-element.22), channel_id=1, source_target_pairs={{0,128},{1,129},{2,130},{3,131},{4,132},{5,133},{6,134},{7,135},{8... | collective-permute-start | bytes 196616 | tf_op jit(solution)/shard_map/ppermute | solution.py:23
  175.6 7.0 %collective-permute-start.36 = (bf16[128,256]{1,0:T(8,128)(2,1)S(1)}, bf16[128,256]{1,0:T(8,128)(2,1)S(1)}, u32[]{:S(2)}, u32[]{:S(2)}) collective-permute-start(bf16[128,256]{1,0:T(8,128)(2,1)S(1)} %get-tuple-element.23), channel_id=1, source_target_pairs={{0,192},{1,193},{2,194},{3,195},{4,196},{5,197},{6,198},{7,199},{8... | collective-permute-start | bytes 196616 | tf_op jit(solution)/shard_map/ppermute | solution.py:23
  182.8 1.3 collective-permute-start.38
where the time goes:
time: 189 us; the launch traced here: 185 us
  waiting for transfers between devices  91.7 us (49%)
  starting transfers between devices  58.6 us (31%)
  matrix products  16.2 us (9%)
  other arithmetic  9.5 us (5%)
  local copies, waits for them, and re-layouts  7.47 us (4%)
    ppermute x39, waiting for transfers between devices, swap(): return lax.ppermute(value, AXES, pairs)  91.7 us
    ppermute x39, starting transfers between devices, swap(): return lax.ppermute(value, AXES, pairs)  58.6 us
    dot_general x8, matrix products, times(): lax.dot_general(piece, w, (((1,), (1,)), ((), ())), preferred_element_typ...  8.79 us
    dot_general x13, matrix products, dot(): return jnp.dot(a, b, preferred_element_type=F32)  7.45 us
    dynamic_slice x3, local copies, waits for them, and re-layouts, own_first(): lax.dynamic_slice_in_dim(w, side * half, half, axis)  5.23 us
    convert_element_type x1, other arithmetic, per_device(): rest = (w_dec - dec.astype(F32)).astype(BF16)  4.2 us
  transfers between devices with their start and end apart: 39, of which 30 were waited for; matrix products, arithmetic and copies ran while one was open for 11% of the time, Pallas kernels for 0%

commit v1 on v0

--- a/solution.py
+++ b/solution.py
@@ -91,7 +91,8 @@
 
 def layer_sum(blocks, c, t):
     half = blocks[0].shape[1] // 2
-    got = swap(jnp.concatenate([block[:, half:] for block in blocks], 0), along_core)
+    early = swap(jnp.concatenate([block[:, half:] for block in blocks[:2]], 0), along_core)
+    got = jnp.concatenate([early, swap(blocks[2][:, half:], along_core)], 0)
     mine = jnp.concatenate([block[:, :half] for block in blocks], 0)
     first = jnp.where(c == 0, mine, got)
     second = jnp.where(c == 0, got, mine)
@@ -143,7 +144,7 @@
     dec_high, dec_low = own_first(dec, 0), own_first(rest, 0)
     acts = gather_rows(acts_two)
     first = dot(acts[0], enc)
-    preact = layer_sum([first] + [dot(piece, enc) for piece in acts[1:]], c, t)
+    preact = layer_sum([first, dot(acts[1], enc), dot(jnp.concatenate(acts[2:], 0), enc)], c, t)
 
     alive = alive_mask.astype(F32)
     alive_half = lax.dynamic_slice_in_dim(alive, c * half, half, 0)
@@ -176,7 +177,7 @@
         return high + low
 
     first = times(remainder[0])
-    summed = layer_sum([first] + [times(piece) for piece in remainder[1:]], c, t) * -alive_half
+    summed = layer_sum([first, times(remainder[1]), times(jnp.concatenate(remainder[2:], 0))], c, t) * -alive_half
     summed = summed.reshape(2, 2, 2, share, half)
     keep = lax.dynamic_index_in_dim(summed, top, 0, keepdims=False)
     give = lax.dynamic_index_in_dim(summed, 1 - top, 0, keepdims=False)

time: 189 us -> 188 us (level)
  waiting for transfers between devices: 91.7 us -> 99.2 us
  matrix products: 16.2 us -> 12.4 us
  local copies, waits for them, and re-layouts: 7.47 us -> 5.42 us
  other arithmetic: 9.5 us -> 7.53 us
    ppermute x39 -> x41, waiting for transfers between devices: 91.7 us -> 99.2 us  [swap(): return lax.ppermute(value, AXES, pairs)]
    dot_general x8 -> x6, matrix products: 8.79 us -> 5.15 us  [times(): lax.dot_general(piece, w, (((1,), (1,)), ((), ())), preferred_element_typ...]
    ppermute x39 -> x41, starting transfers between devices: 58.6 us -> 59.1 us  [swap(): return lax.ppermute(value, AXES, pairs)]
    dot_general x13 -> x12, matrix products: 7.45 us -> 7.28 us  [dot(): return jnp.dot(a, b, preferred_element_type=F32)]
  transfers between devices with their start and end apart: 39 -> 41, of which waited for: 30 -> 32; matrix products, arithmetic and copies ran while one was open for 11% -> 9% of each run, Pallas kernels for 0% -> 0%
where the time goes in v1:
time: 188 us; the launch traced here: 185 us
  waiting for transfers between devices  99.2 us (53%)
  starting transfers between devices  59.1 us (31%)
  matrix products  12.4 us (7%)
  other arithmetic  7.53 us (4%)
  local copies, waits for them, and re-layouts  5.42 us (3%)
    ppermute x41, waiting for transfers between devices, swap(): return lax.ppermute(value, AXES, pairs)  99.2 us
    ppermute x41, starting transfers between devices, swap(): return lax.ppermute(value, AXES, pairs)  59.1 us
    dot_general x12, matrix products, dot(): return jnp.dot(a, b, preferred_element_type=F32)  7.28 us
    dot_general x6, matrix products, times(): lax.dot_general(piece, w, (((1,), (1,)), ((), ())), preferred_element_typ...  5.15 us
  transfers between devices with their start and end apart: 41, of which 32 were waited for; matrix products, arithmetic and copies ran while one was open for 9% of the time, Pallas kernels for 0%

profile of v1, /device:TPU:6, one launch (start us, length us, event | category | flops | bytes accessed | tf_op | source)
XLA Modules:
  0.0 185.0 jit_solution(4222239901738143593)
XLA Ops:
  1.7 1.4 convolution_convert_fusion.6
  5.1 1.5 collective-permute-start.1
  7.1 2.0 %collective-permute-start.2 = (bf16[128,2304]{1,0:T(8,128)(2,1)S(1)}, bf16[128,2304]{1,0:T(8,128)(2,1)S(1)}, u32[]{:S(2)}, u32[]{:S(2)}) collective-permute-start(bf16[128,2304]{1,0:T(8,128)(2,1)S(1)} %convolution_convert_fusion.3), channel_id=1, source_target_pairs={{0,16},{1,17},{2,18},{3,19},{4,20},{5,21},{6,22},{7,23},{8,24},{9,... | collective-permute-start | bytes 1769480 | tf_op jit(solution)/shard_map/ppermute | solution.py:23
  9.0 4.6 %collective-permute-done = bf16[128,2304]{1,0:T(8,128)(2,1)S(1)} collective-permute-done((bf16[128,2304]{1,0:T(8,128)(2,1)S(1)}, bf16[128,2304]{1,0:T(8,128)(2,1)S(1)}, u32[]{:S(2)}, u32[]{:S(2)}) %collective-permute-start) | collective-permute-done | bytes 589856 | tf_op jit(solution)/shard_map/ppermute | solution.py:23
  13.6 9.0 %collective-permute-done.1 = bf16[128,2304]{1,0:T(8,128)(2,1)S(1)} collective-permute-done((bf16[128,2304]{1,0:T(8,128)(2,1)S(1)}, bf16[128,2304]{1,0:T(8,128)(2,1)S(1)}, u32[]{:S(2)}, u32[]{:S(2)}) %collective-permute-start.1) | collective-permute-done | bytes 589856 | tf_op jit(solution)/shard_map/ppermute | solution.py:23
  23.3 1.7 collective-permute-start.3
  24.9 2.9 %collective-permute-start.5 = (bf16[32,2304]{1,0:T(8,128)(2,1)S(1)}, bf16[32,2304]{1,0:T(8,128)(2,1)S(1)}, u32[]{:S(2)}, u32[]{:S(2)}) collective-permute-start(bf16[32,2304]{1,0:T(8,128)(2,1)S(1)} %get-tuple-element.19), channel_id=1, source_target_pairs={{0,4},{1,5},{2,6},{3,7},{4,0},{5,1},{6,2},{7,3},{8,12},{9,13},{10,... | collective-permute-start | bytes 442376 | tf_op jit(solution)/shard_map/ppermute | solution.py:23
  28.5 4.0 %collective-permute-done.5 = bf16[32,2304]{1,0:T(8,128)(2,1)S(1)} collective-permute-done((bf16[32,2304]{1,0:T(8,128)(2,1)S(1)}, bf16[32,2304]{1,0:T(8,128)(2,1)S(1)}, u32[]{:S(2)}, u32[]{:S(2)}) %collective-permute-start.5) | collective-permute-done | bytes 147488 | tf_op jit(solution)/shard_map/ppermute | solution.py:23
  32.5 1.7 collective-permute-done.4
  34.2 2.0 %collective-permute-start.6 = (f32[32,2304]{1,0:T(8,128)S(1)}, f32[32,2304]{1,0:T(8,128)S(1)}, u32[]{:S(2)}, u32[]{:S(2)}) collective-permute-start(f32[32,2304]{1,0:T(8,128)S(1)} %fusion.21), channel_id=1, source_target_pairs={{0,1},{1,0},{2,3},{3,2},{4,5},{5,4},{6,7},{7,6},{8,9},{9,8},{10,11... | collective-permute-start | bytes 884744 | tf_op jit(solution)/shard_map/ppermute | solution.py:23
  36.3 4.8 %collective-permute-done.6 = f32[32,2304]{1,0:T(8,128)S(1)} collective-permute-done((f32[32,2304]{1,0:T(8,128)S(1)}, f32[32,2304]{1,0:T(8,128)S(1)}, u32[]{:S(2)}, u32[]{:S(2)}) %collective-permute-start.6) | collective-permute-done | bytes 294944 | tf_op jit(solution)/shard_map/ppermute | solution.py:23
  42.2 1.7 collective-permute-start.8
  44.7 3.3 %collective-permute-done.9 = bf16[32,2304]{1,0:T(8,128)(2,1)S(1)} collective-permute-done((bf16[32,2304]{1,0:T(8,128)(2,1)S(1)}, bf16[32,2304]{1,0:T(8,128)(2,1)S(1)}, u32[]{:S(2)}, u32[]{:S(2)}) %collective-permute-start.9) | collective-permute-done | bytes 147488 | tf_op jit(solution)/shard_map/ppermute | solution.py:23
  47.9 1.5 collective-permute-done.8
  50.8 1.8 dynamic-slice_bitcast_fusion.1
  53.8 2.9 %collective-permute-start.12 = (bf16[128,2304]{1,0:T(8,128)(2,1)S(1)}, bf16[128,2304]{1,0:T(8,128)(2,1)S(1)}, u32[]{:S(2)}, u32[]{:S(2)}) collective-permute-start(bf16[128,2304]{1,0:T(8,128)(2,1)S(1)} %pad_maximum_fusion.9), channel_id=1, source_target_pairs={{0,16},{1,17},{2,18},{3,19},{4,20},{5,21},{6,22},{7,23},{8,24},{9,... | collective-permute-start | bytes 1769480 | tf_op jit(solution)/shard_map/ppermute | solution.py:23
  57.3 3.4 %collective-permute-done.10 = bf16[128,2304]{1,0:T(8,128)(2,1)S(1)} collective-permute-done((bf16[128,2304]{1,0:T(8,128)(2,1)S(1)}, bf16[128,2304]{1,0:T(8,128)(2,1)S(1)}, u32[]{:S(2)}, u32[]{:S(2)}) %collective-permute-start.10) | collective-permute-done | bytes 589856 | tf_op jit(solution)/shard_map/ppermute | solution.py:23
  61.3 8.8 %collective-permute-done.11 = bf16[128,2304]{1,0:T(8,128)(2,1)S(1)} collective-permute-done((bf16[128,2304]{1,0:T(8,128)(2,1)S(1)}, bf16[128,2304]{1,0:T(8,128)(2,1)S(1)}, u32[]{:S(2)}, u32[]{:S(2)}) %collective-permute-start.11) | collective-permute-done | bytes 589856 | tf_op jit(solution)/shard_map/ppermute | solution.py:23
  71.4 1.4 collective-permute-done.14
  73.0 3.4 %collective-permute-start.15 = (bf16[128,256]{1,0:T(8,128)(2,1)S(1)}, bf16[128,256]{1,0:T(8,128)(2,1)S(1)}, u32[]{:S(2)}, u32[]{:S(2)}) collective-permute-start(bf16[128,256]{1,0:T(8,128)(2,1)S(1)} %get-tuple-element.31), channel_id=1, source_target_pairs={{0,64},{1,65},{2,66},{3,67},{4,68},{5,69},{6,70},{7,71},{8,72},{9,... | collective-permute-start | bytes 196616 | tf_op jit(solution)/shard_map/ppermute | solution.py:23
  76.4 5.4 %collective-permute-start.17 = (bf16[128,256]{1,0:T(8,128)(2,1)S(1)}, bf16[128,256]{1,0:T(8,128)(2,1)S(1)}, u32[]{:S(2)}, u32[]{:S(2)}) collective-permute-start(bf16[128,256]{1,0:T(8,128)(2,1)S(1)} %get-tuple-element.32), channel_id=1, source_target_pairs={{0,128},{1,129},{2,130},{3,131},{4,132},{5,133},{6,134},{7,135},{8... | collective-permute-start | bytes 196616 | tf_op jit(solution)/shard_map/ppermute | solution.py:23
  81.9 3.5 %collective-permute-done.17 = bf16[128,256]{1,0:T(8,128)(2,1)S(1)} collective-permute-done((bf16[128,256]{1,0:T(8,128)(2,1)S(1)}, bf16[128,256]{1,0:T(8,128)(2,1)S(1)}, u32[]{:S(2)}, u32[]{:S(2)}) %collective-permute-start.17) | collective-permute-done | bytes 65568 | tf_op jit(solution)/shard_map/ppermute | solution.py:23
  85.4 2.8 %collective-permute-done.16 = bf16[128,256]{1,0:T(8,128)(2,1)S(1)} collective-permute-done((bf16[128,256]{1,0:T(8,128)(2,1)S(1)}, bf16[128,256]{1,0:T(8,128)(2,1)S(1)}, u32[]{:S(2)}, u32[]{:S(2)}) %collective-permute-start.16) | collective-permute-done | bytes 65568 | tf_op jit(solution)/shard_map/ppermute | solution.py:23
  88.2 3.5 %collective-permute-start.20 = (bf16[128,256]{1,0:T(8,128)(2,1)S(1)}, bf16[128,256]{1,0:T(8,128)(2,1)S(1)}, u32[]{:S(2)}, u32[]{:S(2)}) collective-permute-start(bf16[128,256]{1,0:T(8,128)(2,1)S(1)} %multiply_convert_fusion), channel_id=1, source_target_pairs={{0,128},{1,129},{2,130},{3,131},{4,132},{5,133},{6,134},{7,135},{8... | collective-permute-start | bytes 196616 | tf_op jit(solution)/shard_map/ppermute | solution.py:23
  91.7 2.6 %collective-permute-start.19 = (bf16[128,256]{1,0:T(8,128)(2,1)S(1)}, bf16[128,256]{1,0:T(8,128)(2,1)S(1)}, u32[]{:S(2)}, u32[]{:S(2)}) collective-permute-start(bf16[128,256]{1,0:T(8,128)(2,1)S(1)} %multiply_convert_fusion), channel_id=1, source_target_pairs={{0,192},{1,193},{2,194},{3,195},{4,196},{5,197},{6,198},{7,199},{8... | collective-permute-start | bytes 196616 | tf_op jit(solution)/shard_map/ppermute | solution.py:23
  94.8 2.8 %fusion = (bf16[512,2304]{1,0:T(8,128)(2,1)S(1)}, bf16[512,2304]{1,0:T(8,128)(2,1)S(1)}) fusion(f32[1,512,2304]{2,1,0:T(8,128)} %param.13), kind=kLoop, calls=%fused_computation.2 | loop fusion | flops 4718592 | bytes 9437184 | tf_op jit(solution)/shard_map/convert_element_type | solution.py:143
  98.4 1.7 collective-permute-done.18
  103.6 1.5 collective-permute-start.24
  105.0 2.1 %collective-permute-start.23 = (bf16[128,2304]{1,0:T(8,128)(2,1)S(1)}, bf16[128,2304]{1,0:T(8,128)(2,1)S(1)}, u32[]{:S(2)}, u32[]{:S(2)}) collective-permute-start(bf16[128,2304]{1,0:T(8,128)(2,1)S(1)} %convolution_convert_fusion.1), channel_id=1, source_target_pairs={{0,24},{1,25},{2,26},{3,27},{4,28},{5,29},{6,30},{7,31},{8,16},{9,... | collective-permute-start | bytes 1769480 | tf_op jit(solution)/shard_map/ppermute | solution.py:23
  107.1 8.0 %collective-permute-done.24 = bf16[128,2304]{1,0:T(8,128)(2,1)S(1)} collective-permute-done((bf16[128,2304]{1,0:T(8,128)(2,1)S(1)}, bf16[128,2304]{1,0:T(8,128)(2,1)S(1)}, u32[]{:S(2)}, u32[]{:S(2)}) %collective-permute-start.24) | collective-permute-done | bytes 589856 | tf_op jit(solution)/shard_map/ppermute | solution.py:23
  115.1 6.2 %collective-permute-done.23 = bf16[128,2304]{1,0:T(8,128)(2,1)S(1)} collective-permute-done((bf16[128,2304]{1,0:T(8,128)(2,1)S(1)}, bf16[128,2304]{1,0:T(8,128)(2,1)S(1)}, u32[]{:S(2)}, u32[]{:S(2)}) %collective-permute-start.23) | collective-permute-done | bytes 589856 | tf_op jit(solution)/shard_map/ppermute | solution.py:23
  122.8 1.9 %collective-permute-start.27 = (bf16[32,2304]{1,0:T(8,128)(2,1)S(1)}, bf16[32,2304]{1,0:T(8,128)(2,1)S(1)}, u32[]{:S(2)}, u32[]{:S(2)}) collective-permute-start(bf16[32,2304]{1,0:T(8,128)(2,1)S(1)} %get-tuple-element.16), channel_id=1, source_target_pairs={{0,4},{1,5},{2,6},{3,7},{4,0},{5,1},{6,2},{7,3},{8,12},{9,13},{10,... | collective-permute-start | bytes 442376 | tf_op jit(solution)/shard_map/ppermute | solution.py:23
  124.7 2.1 %collective-permute-start.26 = (bf16[32,2304]{1,0:T(8,128)(2,1)S(1)}, bf16[32,2304]{1,0:T(8,128)(2,1)S(1)}, u32[]{:S(2)}, u32[]{:S(2)}) collective-permute-start(bf16[32,2304]{1,0:T(8,128)(2,1)S(1)} %get-tuple-element.17), channel_id=1, source_target_pairs={{0,6},{1,7},{2,4},{3,5},{4,2},{5,3},{6,0},{7,1},{8,14},{9,15},{10,... | collective-permute-start | bytes 442376 | tf_op jit(solution)/shard_map/ppermute | solution.py:23
  127.2 2.3 %collective-permute-done.27 = bf16[32,2304]{1,0:T(8,128)(2,1)S(1)} collective-permute-done((bf16[32,2304]{1,0:T(8,128)(2,1)S(1)}, bf16[32,2304]{1,0:T(8,128)(2,1)S(1)}, u32[]{:S(2)}, u32[]{:S(2)}) %collective-permute-start.27) | collective-permute-done | bytes 147488 | tf_op jit(solution)/shard_map/ppermute | solution.py:23
  129.5 1.6 collective-permute-done.26
  131.9 1.6 constant_dynamic-slice_fusion.1
  133.6 2.8 %collective-permute-done.28 = bf16[32,2304]{1,0:T(8,128)(2,1)S(1)} collective-permute-done((bf16[32,2304]{1,0:T(8,128)(2,1)S(1)}, bf16[32,2304]{1,0:T(8,128)(2,1)S(1)}, u32[]{:S(2)}, u32[]{:S(2)}) %collective-permute-start.28) | collective-permute-done | bytes 147488 | tf_op jit(solution)/shard_map/ppermute | solution.py:23
  137.6 1.9 %collective-permute-start.31 = (bf16[32,2304]{1,0:T(8,128)(2,1)S(1)}, bf16[32,2304]{1,0:T(8,128)(2,1)S(1)}, u32[]{:S(2)}, u32[]{:S(2)}) collective-permute-start(bf16[32,2304]{1,0:T(8,128)(2,1)S(1)} %get-tuple-element.7), channel_id=1, source_target_pairs={{0,4},{1,5},{2,6},{3,7},{4,0},{5,1},{6,2},{7,3},{8,12},{9,13},{10,... | collective-permute-start | bytes 442376 | tf_op jit(solution)/shard_map/ppermute | solution.py:23
  141.2 3.1 %collective-permute-done.31 = bf16[32,2304]{1,0:T(8,128)(2,1)S(1)} collective-permute-done((bf16[32,2304]{1,0:T(8,128)(2,1)S(1)}, bf16[32,2304]{1,0:T(8,128)(2,1)S(1)}, u32[]{:S(2)}, u32[]{:S(2)}) %collective-permute-start.31) | collective-permute-done | bytes 147488 | tf_op jit(solution)/shard_map/ppermute | solution.py:23
  144.4 1.6 collective-permute-done.30
  146.9 1.4 collective-permute-start.32
  149.4 2.3 %collective-permute-start.33 = (bf16[128,2304]{1,0:T(8,128)(2,1)S(1)}, bf16[128,2304]{1,0:T(8,128)(2,1)S(1)}, u32[]{:S(2)}, u32[]{:S(2)}) collective-permute-start(bf16[128,2304]{1,0:T(8,128)(2,1)S(1)} %pad_maximum_fusion.10), channel_id=1, source_target_pairs={{0,24},{1,25},{2,26},{3,27},{4,28},{5,29},{6,30},{7,31},{8,16},{9,... | collective-permute-start | bytes 1769480 | tf_op jit(solution)/shard_map/ppermute | solution.py:23
  153.9 3.0 %collective-permute-done.32 = bf16[128,2304]{1,0:T(8,128)(2,1)S(1)} collective-permute-done((bf16[128,2304]{1,0:T(8,128)(2,1)S(1)}, bf16[128,2304]{1,0:T(8,128)(2,1)S(1)}, u32[]{:S(2)}, u32[]{:S(2)}) %collective-permute-start.32) | collective-permute-done | bytes 589856 | tf_op jit(solution)/shard_map/ppermute | solution.py:23
  158.8 8.0 %collective-permute-done.33 = bf16[128,2304]{1,0:T(8,128)(2,1)S(1)} collective-permute-done((bf16[128,2304]{1,0:T(8,128)(2,1)S(1)}, bf16[128,2304]{1,0:T(8,128)(2,1)S(1)}, u32[]{:S(2)}, u32[]{:S(2)}) %collective-permute-start.33) | collective-permute-done | bytes 589856 | tf_op jit(solution)/shard_map/ppermute | solution.py:23
  168.7 1.5 collective-permute-done.36
  171.6 4.2 %collective-permute-start.39 = (bf16[128,256]{1,0:T(8,128)(2,1)S(1)}, bf16[128,256]{1,0:T(8,128)(2,1)S(1)}, u32[]{:S(2)}, u32[]{:S(2)}) collective-permute-start(bf16[128,256]{1,0:T(8,128)(2,1)S(1)} %get-tuple-element.22), channel_id=1, source_target_pairs={{0,128},{1,129},{2,130},{3,131},{4,132},{5,133},{6,134},{7,135},{8... | collective-permute-start | bytes 196616 | tf_op jit(solution)/shard_map/ppermute | solution.py:23
  177.7 2.1 %collective-permute-done.39 = bf16[128,256]{1,0:T(8,128)(2,1)S(1)} collective-permute-done((bf16[128,256]{1,0:T(8,128)(2,1)S(1)}, bf16[128,256]{1,0:T(8,128)(2,1)S(1)}, u32[]{:S(2)}, u32[]{:S(2)}) %collective-permute-start.39) | collective-permute-done | bytes 65568 | tf_op jit(solution)/shard_map/ppermute | solution.py:23
  179.9 3.1 %collective-permute-done.38 = bf16[128,256]{1,0:T(8,128)(2,1)S(1)} collective-permute-done((bf16[128,256]{1,0:T(8,128)(2,1)S(1)}, bf16[128,256]{1,0:T(8,128)(2,1)S(1)}, u32[]{:S(2)}, u32[]{:S(2)}) %collective-permute-start.38) | collective-permute-done | bytes 65568 | tf_op jit(solution)/shard_map/ppermute | solution.py:23
  (130 shorter events, 35.8 us)
Async XLA Ops:
  0.6 2.5 %copy-start = (bf16[1,288,2304]{2,1,0:T(8,128)(2,1)S(1)}, bf16[1,288,2304]{2,1,0:T(8,128)(2,1)}, u32[]{:S(2)}) copy-start(bf16[1,288,2304]{2,1,0:T(8,128)(2,1)} %param.10) | copy-start | bytes 3981316
  3.7 10.0 %collective-permute-start = (bf16[128,2304]{1,0:T(8,128)(2,1)S(1)}, bf16[128,2304]{1,0:T(8,128)(2,1)S(1)}, u32[]{:S(2)}, u32[]{:S(2)}) collective-permute-start(bf16[128,2304]{1,0:T(8,128)(2,1)S(1)} %convolution_convert_fusion.5), channel_id=1, source_target_pairs={{0,8},{1,9},{2,10},{3,11},{4,12},{5,13},{6,14},{7,15},{8,0},{9,1},... | collective-permute-start | bytes 1769480 | tf_op jit(solution)/shard_map/ppermute | solution.py:23
  5.1 17.5 %collective-permute-start.1 = (bf16[128,2304]{1,0:T(8,128)(2,1)S(1)}, bf16[128,2304]{1,0:T(8,128)(2,1)S(1)}, u32[]{:S(2)}, u32[]{:S(2)}) collective-permute-start(bf16[128,2304]{1,0:T(8,128)(2,1)S(1)} %convolution_convert_fusion.4), channel_id=1, source_target_pairs={{0,24},{1,25},{2,26},{3,27},{4,28},{5,29},{6,30},{7,31},{8,16},{9,... | collective-permute-start | bytes 1769480 | tf_op jit(solution)/shard_map/ppermute | solution.py:23
  7.1 15.5 %collective-permute-start.2 = (bf16[128,2304]{1,0:T(8,128)(2,1)S(1)}, bf16[128,2304]{1,0:T(8,128)(2,1)S(1)}, u32[]{:S(2)}, u32[]{:S(2)}) collective-permute-start(bf16[128,2304]{1,0:T(8,128)(2,1)S(1)} %convolution_convert_fusion.3), channel_id=1, source_target_pairs={{0,16},{1,17},{2,18},{3,19},{4,20},{5,21},{6,22},{7,23},{8,24},{9,... | collective-permute-start | bytes 1769480 | tf_op jit(solution)/shard_map/ppermute | solution.py:23
  23.3 5.2 %collective-permute-start.3 = (bf16[32,2304]{1,0:T(8,128)(2,1)S(1)}, bf16[32,2304]{1,0:T(8,128)(2,1)S(1)}, u32[]{:S(2)}, u32[]{:S(2)}) collective-permute-start(bf16[32,2304]{1,0:T(8,128)(2,1)S(1)} %get-tuple-element.18), channel_id=1, source_target_pairs={{0,2},{1,3},{2,0},{3,1},{4,6},{5,7},{6,4},{7,5},{8,10},{9,11},{10,... | collective-permute-start | bytes 442376 | tf_op jit(solution)/shard_map/ppermute | solution.py:23
  24.9 7.6 %collective-permute-start.5 = (bf16[32,2304]{1,0:T(8,128)(2,1)S(1)}, bf16[32,2304]{1,0:T(8,128)(2,1)S(1)}, u32[]{:S(2)}, u32[]{:S(2)}) collective-permute-start(bf16[32,2304]{1,0:T(8,128)(2,1)S(1)} %get-tuple-element.19), channel_id=1, source_target_pairs={{0,4},{1,5},{2,6},{3,7},{4,0},{5,1},{6,2},{7,3},{8,12},{9,13},{10,... | collective-permute-start | bytes 442376 | tf_op jit(solution)/shard_map/ppermute | solution.py:23
  27.8 6.4 %collective-permute-start.4 = (bf16[32,2304]{1,0:T(8,128)(2,1)S(1)}, bf16[32,2304]{1,0:T(8,128)(2,1)S(1)}, u32[]{:S(2)}, u32[]{:S(2)}) collective-permute-start(bf16[32,2304]{1,0:T(8,128)(2,1)S(1)} %get-tuple-element.20), channel_id=1, source_target_pairs={{0,6},{1,7},{2,4},{3,5},{4,2},{5,3},{6,0},{7,1},{8,14},{9,15},{10,... | collective-permute-start | bytes 442376 | tf_op jit(solution)/shard_map/ppermute | solution.py:23
  34.2 6.8 %collective-permute-start.6 = (f32[32,2304]{1,0:T(8,128)S(1)}, f32[32,2304]{1,0:T(8,128)S(1)}, u32[]{:S(2)}, u32[]{:S(2)}) collective-permute-start(f32[32,2304]{1,0:T(8,128)S(1)} %fusion.21), channel_id=1, source_target_pairs={{0,1},{1,0},{2,3},{3,2},{4,5},{5,4},{6,7},{7,6},{8,9},{9,8},{10,11... | collective-permute-start | bytes 884744 | tf_op jit(solution)/shard_map/ppermute | solution.py:23
  41.1 6.8 %collective-permute-start.9 = (bf16[32,2304]{1,0:T(8,128)(2,1)S(1)}, bf16[32,2304]{1,0:T(8,128)(2,1)S(1)}, u32[]{:S(2)}, u32[]{:S(2)}) collective-permute-start(bf16[32,2304]{1,0:T(8,128)(2,1)S(1)} %fusion.22), channel_id=1, source_target_pairs={{0,4},{1,5},{2,6},{3,7},{4,0},{5,1},{6,2},{7,3},{8,12},{9,13},{10,... | collective-permute-start | bytes 442376 | tf_op jit(solution)/shard_map/ppermute | solution.py:23
  42.2 7.2 %collective-permute-start.8 = (bf16[32,2304]{1,0:T(8,128)(2,1)S(1)}, bf16[32,2304]{1,0:T(8,128)(2,1)S(1)}, u32[]{:S(2)}, u32[]{:S(2)}) collective-permute-start(bf16[32,2304]{1,0:T(8,128)(2,1)S(1)} %fusion.22), channel_id=1, source_target_pairs={{0,6},{1,7},{2,4},{3,5},{4,2},{5,3},{6,0},{7,1},{8,14},{9,15},{10,... | collective-permute-start | bytes 442376 | tf_op jit(solution)/shard_map/ppermute | solution.py:23
  43.9 6.7 %collective-permute-start.7 = (bf16[32,2304]{1,0:T(8,128)(2,1)S(1)}, bf16[32,2304]{1,0:T(8,128)(2,1)S(1)}, u32[]{:S(2)}, u32[]{:S(2)}) collective-permute-start(bf16[32,2304]{1,0:T(8,128)(2,1)S(1)} %fusion.22), channel_id=1, source_target_pairs={{0,2},{1,3},{2,0},{3,1},{4,6},{5,7},{6,4},{7,5},{8,10},{9,11},{10,... | collective-permute-start | bytes 442376 | tf_op jit(solution)/shard_map/ppermute | solution.py:23
  50.7 10.0 %collective-permute-start.10 = (bf16[128,2304]{1,0:T(8,128)(2,1)S(1)}, bf16[128,2304]{1,0:T(8,128)(2,1)S(1)}, u32[]{:S(2)}, u32[]{:S(2)}) collective-permute-start(bf16[128,2304]{1,0:T(8,128)(2,1)S(1)} %pad_maximum_fusion.9), channel_id=1, source_target_pairs={{0,8},{1,9},{2,10},{3,11},{4,12},{5,13},{6,14},{7,15},{8,0},{9,1},... | collective-permute-start | bytes 1769480 | tf_op jit(solution)/shard_map/ppermute | solution.py:23
  52.6 17.5 %collective-permute-start.11 = (bf16[128,2304]{1,0:T(8,128)(2,1)S(1)}, bf16[128,2304]{1,0:T(8,128)(2,1)S(1)}, u32[]{:S(2)}, u32[]{:S(2)}) collective-permute-start(bf16[128,2304]{1,0:T(8,128)(2,1)S(1)} %pad_maximum_fusion.9), channel_id=1, source_target_pairs={{0,24},{1,25},{2,26},{3,27},{4,28},{5,29},{6,30},{7,31},{8,16},{9,... | collective-permute-start | bytes 1769480 | tf_op jit(solution)/shard_map/ppermute | solution.py:23
  53.8 16.3 %collective-permute-start.12 = (bf16[128,2304]{1,0:T(8,128)(2,1)S(1)}, bf16[128,2304]{1,0:T(8,128)(2,1)S(1)}, u32[]{:S(2)}, u32[]{:S(2)}) collective-permute-start(bf16[128,2304]{1,0:T(8,128)(2,1)S(1)} %pad_maximum_fusion.9), channel_id=1, source_target_pairs={{0,16},{1,17},{2,18},{3,19},{4,20},{5,21},{6,22},{7,23},{8,24},{9,... | collective-permute-start | bytes 1769480 | tf_op jit(solution)/shard_map/ppermute | solution.py:23
  61.2 10.0 %copy-start.8 = (f32[512]{0:T(512)S(1)}, f32[512]{0:T(512)}, u32[]{:S(2)}) copy-start(f32[512]{0:T(512)} %param.12) | copy-start | bytes 6148
  61.2 10.1 %copy-start.7 = (s32[512]{0:T(512)S(1)}, s32[512]{0:T(512)}, u32[]{:S(2)}) copy-start(s32[512]{0:T(512)} %param.15) | copy-start | bytes 6148
  61.2 10.1 %collective-permute-start.13 = (f32[256,256]{1,0:T(8,128)S(1)}, f32[256,256]{1,0:T(8,128)S(1)}, u32[]{:S(2)}, u32[]{:S(2)}) collective-permute-start(f32[256,256]{1,0:T(8,128)S(1)} %pad_maximum_fusion.15), channel_id=1, source_target_pairs={{0,32},{1,33},{2,34},{3,35},{4,36},{5,37},{6,38},{7,39},{8,40},{9,... | collective-permute-start | bytes 786440 | tf_op jit(solution)/shard_map/ppermute | solution.py:23
  70.9 1.8 collective-permute-start.14
  73.0 8.8 %collective-permute-start.15 = (bf16[128,256]{1,0:T(8,128)(2,1)S(1)}, bf16[128,256]{1,0:T(8,128)(2,1)S(1)}, u32[]{:S(2)}, u32[]{:S(2)}) collective-permute-start(bf16[128,256]{1,0:T(8,128)(2,1)S(1)} %get-tuple-element.31), channel_id=1, source_target_pairs={{0,64},{1,65},{2,66},{3,67},{4,68},{5,69},{6,70},{7,71},{8,72},{9,... | collective-permute-start | bytes 196616 | tf_op jit(solution)/shard_map/ppermute | solution.py:23
  76.4 9.0 %collective-permute-start.17 = (bf16[128,256]{1,0:T(8,128)(2,1)S(1)}, bf16[128,256]{1,0:T(8,128)(2,1)S(1)}, u32[]{:S(2)}, u32[]{:S(2)}) collective-permute-start(bf16[128,256]{1,0:T(8,128)(2,1)S(1)} %get-tuple-element.32), channel_id=1, source_target_pairs={{0,128},{1,129},{2,130},{3,131},{4,132},{5,133},{6,134},{7,135},{8... | collective-permute-start | bytes 196616 | tf_op jit(solution)/shard_map/ppermute | solution.py:23
  81.8 6.4 %collective-permute-start.16 = (bf16[128,256]{1,0:T(8,128)(2,1)S(1)}, bf16[128,256]{1,0:T(8,128)(2,1)S(1)}, u32[]{:S(2)}, u32[]{:S(2)}) collective-permute-start(bf16[128,256]{1,0:T(8,128)(2,1)S(1)} %get-tuple-element.33), channel_id=1, source_target_pairs={{0,192},{1,193},{2,194},{3,195},{4,196},{5,197},{6,198},{7,199},{8... | collective-permute-start | bytes 196616 | tf_op jit(solution)/shard_map/ppermute | solution.py:23
  88.2 9.4 %collective-permute-start.20 = (bf16[128,256]{1,0:T(8,128)(2,1)S(1)}, bf16[128,256]{1,0:T(8,128)(2,1)S(1)}, u32[]{:S(2)}, u32[]{:S(2)}) collective-permute-start(bf16[128,256]{1,0:T(8,128)(2,1)S(1)} %multiply_convert_fusion), channel_id=1, source_target_pairs={{0,128},{1,129},{2,130},{3,131},{4,132},{5,133},{6,134},{7,135},{8... | collective-permute-start | bytes 196616 | tf_op jit(solution)/shard_map/ppermute | solution.py:23
  91.7 6.7 %collective-permute-start.19 = (bf16[128,256]{1,0:T(8,128)(2,1)S(1)}, bf16[128,256]{1,0:T(8,128)(2,1)S(1)}, u32[]{:S(2)}, u32[]{:S(2)}) collective-permute-start(bf16[128,256]{1,0:T(8,128)(2,1)S(1)} %multiply_convert_fusion), channel_id=1, source_target_pairs={{0,192},{1,193},{2,194},{3,195},{4,196},{5,197},{6,198},{7,199},{8... | collective-permute-start | bytes 196616 | tf_op jit(solution)/shard_map/ppermute | solution.py:23
  94.3 5.8 %collective-permute-start.18 = (bf16[128,256]{1,0:T(8,128)(2,1)S(1)}, bf16[128,256]{1,0:T(8,128)(2,1)S(1)}, u32[]{:S(2)}, u32[]{:S(2)}) collective-permute-start(bf16[128,256]{1,0:T(8,128)(2,1)S(1)} %multiply_convert_fusion), channel_id=1, source_target_pairs={{0,64},{1,65},{2,66},{3,67},{4,68},{5,69},{6,70},{7,71},{8,72},{9,... | collective-permute-start | bytes 196616 | tf_op jit(solution)/shard_map/ppermute | solution.py:23
  100.1 1.6 collective-permute-start.21
  100.4 21.0 %copy-start.1 = (bf16[256,2304]{1,0:T(8,128)(2,1)}, bf16[256,2304]{1,0:T(8,128)(2,1)S(1)}, u32[]{:S(2)}) copy-start(bf16[256,2304]{1,0:T(8,128)(2,1)S(1)} %get-tuple-element.12) | copy-start | bytes 3538948
  103.6 11.6 %collective-permute-start.24 = (bf16[128,2304]{1,0:T(8,128)(2,1)S(1)}, bf16[128,2304]{1,0:T(8,128)(2,1)S(1)}, u32[]{:S(2)}, u32[]{:S(2)}) collective-permute-start(bf16[128,2304]{1,0:T(8,128)(2,1)S(1)} %convolution_convert_fusion), channel_id=1, source_target_pairs={{0,16},{1,17},{2,18},{3,19},{4,20},{5,21},{6,22},{7,23},{8,24},{9,... | collective-permute-start | bytes 1769480 | tf_op jit(solution)/shard_map/ppermute | solution.py:23
  105.0 16.3 %collective-permute-start.23 = (bf16[128,2304]{1,0:T(8,128)(2,1)S(1)}, bf16[128,2304]{1,0:T(8,128)(2,1)S(1)}, u32[]{:S(2)}, u32[]{:S(2)}) collective-permute-start(bf16[128,2304]{1,0:T(8,128)(2,1)S(1)} %convolution_convert_fusion.1), channel_id=1, source_target_pairs={{0,24},{1,25},{2,26},{3,27},{4,28},{5,29},{6,30},{7,31},{8,16},{9,... | collective-permute-start | bytes 1769480 | tf_op jit(solution)/shard_map/ppermute | solution.py:23
  107.1 14.2 %collective-permute-start.22 = (bf16[128,2304]{1,0:T(8,128)(2,1)S(1)}, bf16[128,2304]{1,0:T(8,128)(2,1)S(1)}, u32[]{:S(2)}, u32[]{:S(2)}) collective-permute-start(bf16[128,2304]{1,0:T(8,128)(2,1)S(1)} %convolution_convert_fusion.2), channel_id=1, source_target_pairs={{0,8},{1,9},{2,10},{3,11},{4,12},{5,13},{6,14},{7,15},{8,0},{9,1},... | collective-permute-start | bytes 1769480 | tf_op jit(solution)/shard_map/ppermute | solution.py:23
  121.9 9.1 %copy-start.5 = (f32[128,2304]{1,0:T(8,128)}, f32[128,2304]{1,0:T(8,128)S(1)}, u32[]{:S(2)}) copy-start(f32[128,2304]{1,0:T(8,128)S(1)} %get-tuple-element.55) | copy-start | bytes 3538948
  122.0 5.2 %collective-permute-start.25 = (bf16[32,2304]{1,0:T(8,128)(2,1)S(1)}, bf16[32,2304]{1,0:T(8,128)(2,1)S(1)}, u32[]{:S(2)}, u32[]{:S(2)}) collective-permute-start(bf16[32,2304]{1,0:T(8,128)(2,1)S(1)} %get-tuple-element.15), channel_id=1, source_target_pairs={{0,2},{1,3},{2,0},{3,1},{4,6},{5,7},{6,4},{7,5},{8,10},{9,11},{10,... | collective-permute-start | bytes 442376 | tf_op jit(solution)/shard_map/ppermute | solution.py:23
  122.8 6.6 %collective-permute-start.27 = (bf16[32,2304]{1,0:T(8,128)(2,1)S(1)}, bf16[32,2304]{1,0:T(8,128)(2,1)S(1)}, u32[]{:S(2)}, u32[]{:S(2)}) collective-permute-start(bf16[32,2304]{1,0:T(8,128)(2,1)S(1)} %get-tuple-element.16), channel_id=1, source_target_pairs={{0,4},{1,5},{2,6},{3,7},{4,0},{5,1},{6,2},{7,3},{8,12},{9,13},{10,... | collective-permute-start | bytes 442376 | tf_op jit(solution)/shard_map/ppermute | solution.py:23
  124.7 6.4 %collective-permute-start.26 = (bf16[32,2304]{1,0:T(8,128)(2,1)S(1)}, bf16[32,2304]{1,0:T(8,128)(2,1)S(1)}, u32[]{:S(2)}, u32[]{:S(2)}) collective-permute-start(bf16[32,2304]{1,0:T(8,128)(2,1)S(1)} %get-tuple-element.17), channel_id=1, source_target_pairs={{0,6},{1,7},{2,4},{3,5},{4,2},{5,3},{6,0},{7,1},{8,14},{9,15},{10,... | collective-permute-start | bytes 442376 | tf_op jit(solution)/shard_map/ppermute | solution.py:23
  131.1 5.2 %collective-permute-start.28 = (bf16[32,2304]{1,0:T(8,128)(2,1)S(1)}, bf16[32,2304]{1,0:T(8,128)(2,1)S(1)}, u32[]{:S(2)}, u32[]{:S(2)}) collective-permute-start(bf16[32,2304]{1,0:T(8,128)(2,1)S(1)} %fusion.45), channel_id=1, source_target_pairs={{0,1},{1,0},{2,3},{3,2},{4,5},{5,4},{6,7},{7,6},{8,9},{9,8},{10,11... | collective-permute-start | bytes 442376 | tf_op jit(solution)/shard_map/ppermute | solution.py:23
  136.4 15.3 %copy-start.3 = (bf16[256,2304]{1,0:T(8,128)(2,1)S(1)}, bf16[256,2304]{1,0:T(8,128)(2,1)}, u32[]{:S(2)}) copy-start(bf16[256,2304]{1,0:T(8,128)(2,1)} %get-tuple-element.9) | copy-start | bytes 3538948
  136.4 15.3 %copy-start.4 = (bf16[256,2304]{1,0:T(8,128)(2,1)S(1)}, bf16[256,2304]{1,0:T(8,128)(2,1)}, u32[]{:S(2)}) copy-start(bf16[256,2304]{1,0:T(8,128)(2,1)} %get-tuple-element.10) | copy-start | bytes 3538948
  137.6 6.7 %collective-permute-start.31 = (bf16[32,2304]{1,0:T(8,128)(2,1)S(1)}, bf16[32,2304]{1,0:T(8,128)(2,1)S(1)}, u32[]{:S(2)}, u32[]{:S(2)}) collective-permute-start(bf16[32,2304]{1,0:T(8,128)(2,1)S(1)} %get-tuple-element.7), channel_id=1, source_target_pairs={{0,4},{1,5},{2,6},{3,7},{4,0},{5,1},{6,2},{7,3},{8,12},{9,13},{10,... | collective-permute-start | bytes 442376 | tf_op jit(solution)/shard_map/ppermute | solution.py:23
  139.6 6.4 %collective-permute-start.30 = (bf16[32,2304]{1,0:T(8,128)(2,1)S(1)}, bf16[32,2304]{1,0:T(8,128)(2,1)S(1)}, u32[]{:S(2)}, u32[]{:S(2)}) collective-permute-start(bf16[32,2304]{1,0:T(8,128)(2,1)S(1)} %get-tuple-element.7), channel_id=1, source_target_pairs={{0,6},{1,7},{2,4},{3,5},{4,2},{5,3},{6,0},{7,1},{8,14},{9,15},{10,... | collective-permute-start | bytes 442376 | tf_op jit(solution)/shard_map/ppermute | solution.py:23
  140.6 6.2 %collective-permute-start.29 = (bf16[32,2304]{1,0:T(8,128)(2,1)S(1)}, bf16[32,2304]{1,0:T(8,128)(2,1)S(1)}, u32[]{:S(2)}, u32[]{:S(2)}) collective-permute-start(bf16[32,2304]{1,0:T(8,128)(2,1)S(1)} %get-tuple-element.7), channel_id=1, source_target_pairs={{0,2},{1,3},{2,0},{3,1},{4,6},{5,7},{6,4},{7,5},{8,10},{9,11},{10,... | collective-permute-start | bytes 442376 | tf_op jit(solution)/shard_map/ppermute | solution.py:23
  146.9 10.0 %collective-permute-start.32 = (bf16[128,2304]{1,0:T(8,128)(2,1)S(1)}, bf16[128,2304]{1,0:T(8,128)(2,1)S(1)}, u32[]{:S(2)}, u32[]{:S(2)}) collective-permute-start(bf16[128,2304]{1,0:T(8,128)(2,1)S(1)} %pad_maximum_fusion.10), channel_id=1, source_target_pairs={{0,8},{1,9},{2,10},{3,11},{4,12},{5,13},{6,14},{7,15},{8,0},{9,1},... | collective-permute-start | bytes 1769480 | tf_op jit(solution)/shard_map/ppermute | solution.py:23
  148.3 18.6 %collective-permute-start.34 = (bf16[128,2304]{1,0:T(8,128)(2,1)S(1)}, bf16[128,2304]{1,0:T(8,128)(2,1)S(1)}, u32[]{:S(2)}, u32[]{:S(2)}) collective-permute-start(bf16[128,2304]{1,0:T(8,128)(2,1)S(1)} %pad_maximum_fusion.10), channel_id=1, source_target_pairs={{0,16},{1,17},{2,18},{3,19},{4,20},{5,21},{6,22},{7,23},{8,24},{9,... | collective-permute-start | bytes 1769480 | tf_op jit(solution)/shard_map/ppermute | solution.py:23
  149.4 17.4 %collective-permute-start.33 = (bf16[128,2304]{1,0:T(8,128)(2,1)S(1)}, bf16[128,2304]{1,0:T(8,128)(2,1)S(1)}, u32[]{:S(2)}, u32[]{:S(2)}) collective-permute-start(bf16[128,2304]{1,0:T(8,128)(2,1)S(1)} %pad_maximum_fusion.10), channel_id=1, source_target_pairs={{0,24},{1,25},{2,26},{3,27},{4,28},{5,29},{6,30},{7,31},{8,16},{9,... | collective-permute-start | bytes 1769480 | tf_op jit(solution)/shard_map/ppermute | solution.py:23
  158.7 10.0 %collective-permute-start.35 = (f32[256,256]{1,0:T(8,128)S(1)}, f32[256,256]{1,0:T(8,128)S(1)}, u32[]{:S(2)}, u32[]{:S(2)}) collective-permute-start(f32[256,256]{1,0:T(8,128)S(1)} %pad_maximum_fusion.17), channel_id=1, source_target_pairs={{0,32},{1,33},{2,34},{3,35},{4,36},{5,37},{6,38},{7,39},{8,40},{9,... | collective-permute-start | bytes 786440 | tf_op jit(solution)/shard_map/ppermute | solution.py:23
  168.6 1.6 collective-permute-start.36
  170.5 7.2 %collective-permute-start.37 = (bf16[128,256]{1,0:T(8,128)(2,1)S(1)}, bf16[128,256]{1,0:T(8,128)(2,1)S(1)}, u32[]{:S(2)}, u32[]{:S(2)}) collective-permute-start(bf16[128,256]{1,0:T(8,128)(2,1)S(1)} %get-tuple-element.21), channel_id=1, source_target_pairs={{0,64},{1,65},{2,66},{3,67},{4,68},{5,69},{6,70},{7,71},{8,72},{9,... | collective-permute-start | bytes 196616 | tf_op jit(solution)/shard_map/ppermute | solution.py:23
  171.6 8.3 %collective-permute-start.39 = (bf16[128,256]{1,0:T(8,128)(2,1)S(1)}, bf16[128,256]{1,0:T(8,128)(2,1)S(1)}, u32[]{:S(2)}, u32[]{:S(2)}) collective-permute-start(bf16[128,256]{1,0:T(8,128)(2,1)S(1)} %get-tuple-element.22), channel_id=1, source_target_pairs={{0,128},{1,129},{2,130},{3,131},{4,132},{5,133},{6,134},{7,135},{8... | collective-permute-start | bytes 196616 | tf_op jit(solution)/shard_map/ppermute | solution.py:23
  175.8 7.1 %collective-permute-start.38 = (bf16[128,256]{1,0:T(8,128)(2,1)S(1)}, bf16[128,256]{1,0:T(8,128)(2,1)S(1)}, u32[]{:S(2)}, u32[]{:S(2)}) collective-permute-start(bf16[128,256]{1,0:T(8,128)(2,1)S(1)} %get-tuple-element.23), channel_id=1, source_target_pairs={{0,192},{1,193},{2,194},{3,195},{4,196},{5,197},{6,198},{7,199},{8... | collective-permute-start | bytes 196616 | tf_op jit(solution)/shard_map/ppermute | solution.py:23
  183.0 1.3 collective-permute-start.40
  (2 other events, 2.9 us)

commit v2 on v1

--- a/solution.py
+++ b/solution.py
@@ -150,8 +150,10 @@
     alive_half = lax.dynamic_slice_in_dim(alive, c * half, half, 0)
     bias_half = lax.dynamic_slice_in_dim(b_enc, c * half, half, 0)
     lat = (jnp.maximum(preact + bias_half, 0.0) * alive_half).astype(BF16)
-    side = jnp.concatenate([lat] + [swap(lat, along_zh(gray(s))) for s in SLOTS], 0)
-    wide = jnp.concatenate([side, swap(side, along_core)], 1)
+    pieces = [lat] + [swap(lat, along_zh(gray(s))) for s in SLOTS]
+    side = jnp.concatenate(pieces, 0)
+    other = jnp.concatenate([swap(lat, along_core), swap(jnp.concatenate(pieces[1:], 0), along_core)], 0)
+    wide = jnp.concatenate([side, other], 1)
     top = c ^ (y >> 1)
 
     def all_latents(a):

time: 188 us -> 188 us (level)
    ppermute x41 -> x42, starting transfers between devices: 59.1 us -> 59.4 us  [swap(): return lax.ppermute(value, AXES, pairs)]
    ppermute x41 -> x42, waiting for transfers between devices: 99.2 us -> 99.1 us  [swap(): return lax.ppermute(value, AXES, pairs)]
  transfers between devices with their start and end apart: 41 -> 42, of which waited for: 32 -> 32; matrix products, arithmetic and copies ran while one was open for 9% -> 9% of each run, Pallas kernels for 0% -> 0%
where the time goes in v2:
time: 188 us; the launch traced here: 185 us
  waiting for transfers between devices  99.1 us (53%)
  starting transfers between devices  59.4 us (32%)
  matrix products  12.4 us (7%)
  other arithmetic  7.51 us (4%)
  local copies, waits for them, and re-layouts  5.42 us (3%)
    ppermute x42, waiting for transfers between devices, swap(): return lax.ppermute(value, AXES, pairs)  99.1 us
    ppermute x42, starting transfers between devices, swap(): return lax.ppermute(value, AXES, pairs)  59.4 us
    dot_general x12, matrix products, dot(): return jnp.dot(a, b, preferred_element_type=F32)  7.27 us
    dot_general x6, matrix products, times(): lax.dot_general(piece, w, (((1,), (1,)), ((), ())), preferred_element_typ...  5.14 us
  transfers between devices with their start and end apart: 42, of which 32 were waited for; matrix products, arithmetic and copies ran while one was open for 9% of the time, Pallas kernels for 0%

profile of v2, /device:TPU:6, one launch (start us, length us, event | category | flops | bytes accessed | tf_op | source)
XLA Modules:
  0.0 185.2 jit_solution(12996303395155717480)
XLA Ops:
  1.7 1.4 convolution_convert_fusion.6
  5.1 1.5 collective-permute-start.1
  7.1 2.0 %collective-permute-start.2 = (bf16[128,2304]{1,0:T(8,128)(2,1)S(1)}, bf16[128,2304]{1,0:T(8,128)(2,1)S(1)}, u32[]{:S(2)}, u32[]{:S(2)}) collective-permute-start(bf16[128,2304]{1,0:T(8,128)(2,1)S(1)} %convolution_convert_fusion.3), channel_id=1, source_target_pairs={{0,16},{1,17},{2,18},{3,19},{4,20},{5,21},{6,22},{7,23},{8,24},{9,... | collective-permute-start | bytes 1769480 | tf_op jit(solution)/shard_map/ppermute | solution.py:23
  9.0 4.6 %collective-permute-done = bf16[128,2304]{1,0:T(8,128)(2,1)S(1)} collective-permute-done((bf16[128,2304]{1,0:T(8,128)(2,1)S(1)}, bf16[128,2304]{1,0:T(8,128)(2,1)S(1)}, u32[]{:S(2)}, u32[]{:S(2)}) %collective-permute-start) | collective-permute-done | bytes 589856 | tf_op jit(solution)/shard_map/ppermute | solution.py:23
  13.6 9.0 %collective-permute-done.1 = bf16[128,2304]{1,0:T(8,128)(2,1)S(1)} collective-permute-done((bf16[128,2304]{1,0:T(8,128)(2,1)S(1)}, bf16[128,2304]{1,0:T(8,128)(2,1)S(1)}, u32[]{:S(2)}, u32[]{:S(2)}) %collective-permute-start.1) | collective-permute-done | bytes 589856 | tf_op jit(solution)/shard_map/ppermute | solution.py:23
  23.3 1.7 collective-permute-start.3
  24.9 2.9 %collective-permute-start.5 = (bf16[32,2304]{1,0:T(8,128)(2,1)S(1)}, bf16[32,2304]{1,0:T(8,128)(2,1)S(1)}, u32[]{:S(2)}, u32[]{:S(2)}) collective-permute-start(bf16[32,2304]{1,0:T(8,128)(2,1)S(1)} %get-tuple-element.19), channel_id=1, source_target_pairs={{0,4},{1,5},{2,6},{3,7},{4,0},{5,1},{6,2},{7,3},{8,12},{9,13},{10,... | collective-permute-start | bytes 442376 | tf_op jit(solution)/shard_map/ppermute | solution.py:23
  28.5 4.0 %collective-permute-done.5 = bf16[32,2304]{1,0:T(8,128)(2,1)S(1)} collective-permute-done((bf16[32,2304]{1,0:T(8,128)(2,1)S(1)}, bf16[32,2304]{1,0:T(8,128)(2,1)S(1)}, u32[]{:S(2)}, u32[]{:S(2)}) %collective-permute-start.5) | collective-permute-done | bytes 147488 | tf_op jit(solution)/shard_map/ppermute | solution.py:23
  32.5 1.7 collective-permute-done.4
  34.2 2.0 %collective-permute-start.6 = (f32[32,2304]{1,0:T(8,128)S(1)}, f32[32,2304]{1,0:T(8,128)S(1)}, u32[]{:S(2)}, u32[]{:S(2)}) collective-permute-start(f32[32,2304]{1,0:T(8,128)S(1)} %fusion.21), channel_id=1, source_target_pairs={{0,1},{1,0},{2,3},{3,2},{4,5},{5,4},{6,7},{7,6},{8,9},{9,8},{10,11... | collective-permute-start | bytes 884744 | tf_op jit(solution)/shard_map/ppermute | solution.py:23
  36.3 4.8 %collective-permute-done.6 = f32[32,2304]{1,0:T(8,128)S(1)} collective-permute-done((f32[32,2304]{1,0:T(8,128)S(1)}, f32[32,2304]{1,0:T(8,128)S(1)}, u32[]{:S(2)}, u32[]{:S(2)}) %collective-permute-start.6) | collective-permute-done | bytes 294944 | tf_op jit(solution)/shard_map/ppermute | solution.py:23
  42.2 1.7 collective-permute-start.8
  44.7 3.3 %collective-permute-done.9 = bf16[32,2304]{1,0:T(8,128)(2,1)S(1)} collective-permute-done((bf16[32,2304]{1,0:T(8,128)(2,1)S(1)}, bf16[32,2304]{1,0:T(8,128)(2,1)S(1)}, u32[]{:S(2)}, u32[]{:S(2)}) %collective-permute-start.9) | collective-permute-done | bytes 147488 | tf_op jit(solution)/shard_map/ppermute | solution.py:23
  47.9 1.5 collective-permute-done.8
  50.8 1.8 dynamic-slice_bitcast_fusion.1
  53.8 2.9 %collective-permute-start.12 = (bf16[128,2304]{1,0:T(8,128)(2,1)S(1)}, bf16[128,2304]{1,0:T(8,128)(2,1)S(1)}, u32[]{:S(2)}, u32[]{:S(2)}) collective-permute-start(bf16[128,2304]{1,0:T(8,128)(2,1)S(1)} %pad_maximum_fusion.9), channel_id=1, source_target_pairs={{0,16},{1,17},{2,18},{3,19},{4,20},{5,21},{6,22},{7,23},{8,24},{9,... | collective-permute-start | bytes 1769480 | tf_op jit(solution)/shard_map/ppermute | solution.py:23
  57.3 3.4 %collective-permute-done.10 = bf16[128,2304]{1,0:T(8,128)(2,1)S(1)} collective-permute-done((bf16[128,2304]{1,0:T(8,128)(2,1)S(1)}, bf16[128,2304]{1,0:T(8,128)(2,1)S(1)}, u32[]{:S(2)}, u32[]{:S(2)}) %collective-permute-start.10) | collective-permute-done | bytes 589856 | tf_op jit(solution)/shard_map/ppermute | solution.py:23
  61.3 8.8 %collective-permute-done.11 = bf16[128,2304]{1,0:T(8,128)(2,1)S(1)} collective-permute-done((bf16[128,2304]{1,0:T(8,128)(2,1)S(1)}, bf16[128,2304]{1,0:T(8,128)(2,1)S(1)}, u32[]{:S(2)}, u32[]{:S(2)}) %collective-permute-start.11) | collective-permute-done | bytes 589856 | tf_op jit(solution)/shard_map/ppermute | solution.py:23
  71.4 1.4 collective-permute-done.14
  73.0 3.4 %collective-permute-start.15 = (bf16[128,256]{1,0:T(8,128)(2,1)S(1)}, bf16[128,256]{1,0:T(8,128)(2,1)S(1)}, u32[]{:S(2)}, u32[]{:S(2)}) collective-permute-start(bf16[128,256]{1,0:T(8,128)(2,1)S(1)} %get-tuple-element.31), channel_id=1, source_target_pairs={{0,64},{1,65},{2,66},{3,67},{4,68},{5,69},{6,70},{7,71},{8,72},{9,... | collective-permute-start | bytes 196616 | tf_op jit(solution)/shard_map/ppermute | solution.py:23
  76.4 5.4 %collective-permute-start.17 = (bf16[128,256]{1,0:T(8,128)(2,1)S(1)}, bf16[128,256]{1,0:T(8,128)(2,1)S(1)}, u32[]{:S(2)}, u32[]{:S(2)}) collective-permute-start(bf16[128,256]{1,0:T(8,128)(2,1)S(1)} %get-tuple-element.32), channel_id=1, source_target_pairs={{0,128},{1,129},{2,130},{3,131},{4,132},{5,133},{6,134},{7,135},{8... | collective-permute-start | bytes 196616 | tf_op jit(solution)/shard_map/ppermute | solution.py:23
  81.9 3.5 %collective-permute-done.17 = bf16[128,256]{1,0:T(8,128)(2,1)S(1)} collective-permute-done((bf16[128,256]{1,0:T(8,128)(2,1)S(1)}, bf16[128,256]{1,0:T(8,128)(2,1)S(1)}, u32[]{:S(2)}, u32[]{:S(2)}) %collective-permute-start.17) | collective-permute-done | bytes 65568 | tf_op jit(solution)/shard_map/ppermute | solution.py:23
  85.4 2.8 %collective-permute-done.16 = bf16[128,256]{1,0:T(8,128)(2,1)S(1)} collective-permute-done((bf16[128,256]{1,0:T(8,128)(2,1)S(1)}, bf16[128,256]{1,0:T(8,128)(2,1)S(1)}, u32[]{:S(2)}, u32[]{:S(2)}) %collective-permute-start.16) | collective-permute-done | bytes 65568 | tf_op jit(solution)/shard_map/ppermute | solution.py:23
  88.2 3.5 %collective-permute-start.20 = (bf16[128,256]{1,0:T(8,128)(2,1)S(1)}, bf16[128,256]{1,0:T(8,128)(2,1)S(1)}, u32[]{:S(2)}, u32[]{:S(2)}) collective-permute-start(bf16[128,256]{1,0:T(8,128)(2,1)S(1)} %multiply_convert_fusion), channel_id=1, source_target_pairs={{0,128},{1,129},{2,130},{3,131},{4,132},{5,133},{6,134},{7,135},{8... | collective-permute-start | bytes 196616 | tf_op jit(solution)/shard_map/ppermute | solution.py:23
  91.7 2.6 %collective-permute-start.19 = (bf16[128,256]{1,0:T(8,128)(2,1)S(1)}, bf16[128,256]{1,0:T(8,128)(2,1)S(1)}, u32[]{:S(2)}, u32[]{:S(2)}) collective-permute-start(bf16[128,256]{1,0:T(8,128)(2,1)S(1)} %multiply_convert_fusion), channel_id=1, source_target_pairs={{0,192},{1,193},{2,194},{3,195},{4,196},{5,197},{6,198},{7,199},{8... | collective-permute-start | bytes 196616 | tf_op jit(solution)/shard_map/ppermute | solution.py:23
  94.8 2.8 %fusion = (bf16[512,2304]{1,0:T(8,128)(2,1)S(1)}, bf16[512,2304]{1,0:T(8,128)(2,1)S(1)}) fusion(f32[1,512,2304]{2,1,0:T(8,128)} %param.13), kind=kLoop, calls=%fused_computation.2 | loop fusion | flops 4718592 | bytes 9437184 | tf_op jit(solution)/shard_map/convert_element_type | solution.py:143
  98.4 1.7 collective-permute-done.18
  103.5 1.5 collective-permute-start.25
  104.9 2.1 %collective-permute-start.24 = (bf16[128,2304]{1,0:T(8,128)(2,1)S(1)}, bf16[128,2304]{1,0:T(8,128)(2,1)S(1)}, u32[]{:S(2)}, u32[]{:S(2)}) collective-permute-start(bf16[128,2304]{1,0:T(8,128)(2,1)S(1)} %convolution_convert_fusion.1), channel_id=1, source_target_pairs={{0,24},{1,25},{2,26},{3,27},{4,28},{5,29},{6,30},{7,31},{8,16},{9,... | collective-permute-start | bytes 1769480 | tf_op jit(solution)/shard_map/ppermute | solution.py:23
  107.0 8.0 %collective-permute-done.25 = bf16[128,2304]{1,0:T(8,128)(2,1)S(1)} collective-permute-done((bf16[128,2304]{1,0:T(8,128)(2,1)S(1)}, bf16[128,2304]{1,0:T(8,128)(2,1)S(1)}, u32[]{:S(2)}, u32[]{:S(2)}) %collective-permute-start.25) | collective-permute-done | bytes 589856 | tf_op jit(solution)/shard_map/ppermute | solution.py:23
  115.0 6.2 %collective-permute-done.24 = bf16[128,2304]{1,0:T(8,128)(2,1)S(1)} collective-permute-done((bf16[128,2304]{1,0:T(8,128)(2,1)S(1)}, bf16[128,2304]{1,0:T(8,128)(2,1)S(1)}, u32[]{:S(2)}, u32[]{:S(2)}) %collective-permute-start.24) | collective-permute-done | bytes 589856 | tf_op jit(solution)/shard_map/ppermute | solution.py:23
  122.7 1.9 %collective-permute-start.28 = (bf16[32,2304]{1,0:T(8,128)(2,1)S(1)}, bf16[32,2304]{1,0:T(8,128)(2,1)S(1)}, u32[]{:S(2)}, u32[]{:S(2)}) collective-permute-start(bf16[32,2304]{1,0:T(8,128)(2,1)S(1)} %get-tuple-element.16), channel_id=1, source_target_pairs={{0,4},{1,5},{2,6},{3,7},{4,0},{5,1},{6,2},{7,3},{8,12},{9,13},{10,... | collective-permute-start | bytes 442376 | tf_op jit(solution)/shard_map/ppermute | solution.py:23
  124.6 2.1 %collective-permute-start.27 = (bf16[32,2304]{1,0:T(8,128)(2,1)S(1)}, bf16[32,2304]{1,0:T(8,128)(2,1)S(1)}, u32[]{:S(2)}, u32[]{:S(2)}) collective-permute-start(bf16[32,2304]{1,0:T(8,128)(2,1)S(1)} %get-tuple-element.17), channel_id=1, source_target_pairs={{0,6},{1,7},{2,4},{3,5},{4,2},{5,3},{6,0},{7,1},{8,14},{9,15},{10,... | collective-permute-start | bytes 442376 | tf_op jit(solution)/shard_map/ppermute | solution.py:23
  127.1 2.3 %collective-permute-done.28 = bf16[32,2304]{1,0:T(8,128)(2,1)S(1)} collective-permute-done((bf16[32,2304]{1,0:T(8,128)(2,1)S(1)}, bf16[32,2304]{1,0:T(8,128)(2,1)S(1)}, u32[]{:S(2)}, u32[]{:S(2)}) %collective-permute-start.28) | collective-permute-done | bytes 147488 | tf_op jit(solution)/shard_map/ppermute | solution.py:23
  129.4 1.6 collective-permute-done.27
  131.8 1.6 constant_dynamic-slice_fusion.1
  133.5 2.8 %collective-permute-done.29 = bf16[32,2304]{1,0:T(8,128)(2,1)S(1)} collective-permute-done((bf16[32,2304]{1,0:T(8,128)(2,1)S(1)}, bf16[32,2304]{1,0:T(8,128)(2,1)S(1)}, u32[]{:S(2)}, u32[]{:S(2)}) %collective-permute-start.29) | collective-permute-done | bytes 147488 | tf_op jit(solution)/shard_map/ppermute | solution.py:23
  137.5 2.2 %collective-permute-start.32 = (bf16[32,2304]{1,0:T(8,128)(2,1)S(1)}, bf16[32,2304]{1,0:T(8,128)(2,1)S(1)}, u32[]{:S(2)}, u32[]{:S(2)}) collective-permute-start(bf16[32,2304]{1,0:T(8,128)(2,1)S(1)} %get-tuple-element.7), channel_id=1, source_target_pairs={{0,4},{1,5},{2,6},{3,7},{4,0},{5,1},{6,2},{7,3},{8,12},{9,13},{10,... | collective-permute-start | bytes 442376 | tf_op jit(solution)/shard_map/ppermute | solution.py:23
  141.4 3.1 %collective-permute-done.32 = bf16[32,2304]{1,0:T(8,128)(2,1)S(1)} collective-permute-done((bf16[32,2304]{1,0:T(8,128)(2,1)S(1)}, bf16[32,2304]{1,0:T(8,128)(2,1)S(1)}, u32[]{:S(2)}, u32[]{:S(2)}) %collective-permute-start.32) | collective-permute-done | bytes 147488 | tf_op jit(solution)/shard_map/ppermute | solution.py:23
  144.5 1.6 collective-permute-done.31
  147.0 1.4 collective-permute-start.33
  149.6 2.2 %collective-permute-start.34 = (bf16[128,2304]{1,0:T(8,128)(2,1)S(1)}, bf16[128,2304]{1,0:T(8,128)(2,1)S(1)}, u32[]{:S(2)}, u32[]{:S(2)}) collective-permute-start(bf16[128,2304]{1,0:T(8,128)(2,1)S(1)} %pad_maximum_fusion.10), channel_id=1, source_target_pairs={{0,24},{1,25},{2,26},{3,27},{4,28},{5,29},{6,30},{7,31},{8,16},{9,... | collective-permute-start | bytes 1769480 | tf_op jit(solution)/shard_map/ppermute | solution.py:23
  154.0 3.0 %collective-permute-done.33 = bf16[128,2304]{1,0:T(8,128)(2,1)S(1)} collective-permute-done((bf16[128,2304]{1,0:T(8,128)(2,1)S(1)}, bf16[128,2304]{1,0:T(8,128)(2,1)S(1)}, u32[]{:S(2)}, u32[]{:S(2)}) %collective-permute-start.33) | collective-permute-done | bytes 589856 | tf_op jit(solution)/shard_map/ppermute | solution.py:23
  158.9 8.0 %collective-permute-done.34 = bf16[128,2304]{1,0:T(8,128)(2,1)S(1)} collective-permute-done((bf16[128,2304]{1,0:T(8,128)(2,1)S(1)}, bf16[128,2304]{1,0:T(8,128)(2,1)S(1)}, u32[]{:S(2)}, u32[]{:S(2)}) %collective-permute-start.34) | collective-permute-done | bytes 589856 | tf_op jit(solution)/shard_map/ppermute | solution.py:23
  168.9 1.5 collective-permute-done.37
  171.8 4.2 %collective-permute-start.40 = (bf16[128,256]{1,0:T(8,128)(2,1)S(1)}, bf16[128,256]{1,0:T(8,128)(2,1)S(1)}, u32[]{:S(2)}, u32[]{:S(2)}) collective-permute-start(bf16[128,256]{1,0:T(8,128)(2,1)S(1)} %get-tuple-element.22), channel_id=1, source_target_pairs={{0,128},{1,129},{2,130},{3,131},{4,132},{5,133},{6,134},{7,135},{8... | collective-permute-start | bytes 196616 | tf_op jit(solution)/shard_map/ppermute | solution.py:23
  177.9 2.1 %collective-permute-done.40 = bf16[128,256]{1,0:T(8,128)(2,1)S(1)} collective-permute-done((bf16[128,256]{1,0:T(8,128)(2,1)S(1)}, bf16[128,256]{1,0:T(8,128)(2,1)S(1)}, u32[]{:S(2)}, u32[]{:S(2)}) %collective-permute-start.40) | collective-permute-done | bytes 65568 | tf_op jit(solution)/shard_map/ppermute | solution.py:23
  180.0 3.0 %collective-permute-done.39 = bf16[128,256]{1,0:T(8,128)(2,1)S(1)} collective-permute-done((bf16[128,256]{1,0:T(8,128)(2,1)S(1)}, bf16[128,256]{1,0:T(8,128)(2,1)S(1)}, u32[]{:S(2)}, u32[]{:S(2)}) %collective-permute-start.39) | collective-permute-done | bytes 65568 | tf_op jit(solution)/shard_map/ppermute | solution.py:23
  (132 shorter events, 35.7 us)
Async XLA Ops:
  3.7 10.0 %collective-permute-start = (bf16[128,2304]{1,0:T(8,128)(2,1)S(1)}, bf16[128,2304]{1,0:T(8,128)(2,1)S(1)}, u32[]{:S(2)}, u32[]{:S(2)}) collective-permute-start(bf16[128,2304]{1,0:T(8,128)(2,1)S(1)} %convolution_convert_fusion.5), channel_id=1, source_target_pairs={{0,8},{1,9},{2,10},{3,11},{4,12},{5,13},{6,14},{7,15},{8,0},{9,1},... | collective-permute-start | bytes 1769480 | tf_op jit(solution)/shard_map/ppermute | solution.py:23
  5.1 17.5 %collective-permute-start.1 = (bf16[128,2304]{1,0:T(8,128)(2,1)S(1)}, bf16[128,2304]{1,0:T(8,128)(2,1)S(1)}, u32[]{:S(2)}, u32[]{:S(2)}) collective-permute-start(bf16[128,2304]{1,0:T(8,128)(2,1)S(1)} %convolution_convert_fusion.4), channel_id=1, source_target_pairs={{0,24},{1,25},{2,26},{3,27},{4,28},{5,29},{6,30},{7,31},{8,16},{9,... | collective-permute-start | bytes 1769480 | tf_op jit(solution)/shard_map/ppermute | solution.py:23
  7.1 15.5 %collective-permute-start.2 = (bf16[128,2304]{1,0:T(8,128)(2,1)S(1)}, bf16[128,2304]{1,0:T(8,128)(2,1)S(1)}, u32[]{:S(2)}, u32[]{:S(2)}) collective-permute-start(bf16[128,2304]{1,0:T(8,128)(2,1)S(1)} %convolution_convert_fusion.3), channel_id=1, source_target_pairs={{0,16},{1,17},{2,18},{3,19},{4,20},{5,21},{6,22},{7,23},{8,24},{9,... | collective-permute-start | bytes 1769480 | tf_op jit(solution)/shard_map/ppermute | solution.py:23
  23.3 5.2 %collective-permute-start.3 = (bf16[32,2304]{1,0:T(8,128)(2,1)S(1)}, bf16[32,2304]{1,0:T(8,128)(2,1)S(1)}, u32[]{:S(2)}, u32[]{:S(2)}) collective-permute-start(bf16[32,2304]{1,0:T(8,128)(2,1)S(1)} %get-tuple-element.18), channel_id=1, source_target_pairs={{0,2},{1,3},{2,0},{3,1},{4,6},{5,7},{6,4},{7,5},{8,10},{9,11},{10,... | collective-permute-start | bytes 442376 | tf_op jit(solution)/shard_map/ppermute | solution.py:23
  24.9 7.6 %collective-permute-start.5 = (bf16[32,2304]{1,0:T(8,128)(2,1)S(1)}, bf16[32,2304]{1,0:T(8,128)(2,1)S(1)}, u32[]{:S(2)}, u32[]{:S(2)}) collective-permute-start(bf16[32,2304]{1,0:T(8,128)(2,1)S(1)} %get-tuple-element.19), channel_id=1, source_target_pairs={{0,4},{1,5},{2,6},{3,7},{4,0},{5,1},{6,2},{7,3},{8,12},{9,13},{10,... | collective-permute-start | bytes 442376 | tf_op jit(solution)/shard_map/ppermute | solution.py:23
  27.8 6.4 %collective-permute-start.4 = (bf16[32,2304]{1,0:T(8,128)(2,1)S(1)}, bf16[32,2304]{1,0:T(8,128)(2,1)S(1)}, u32[]{:S(2)}, u32[]{:S(2)}) collective-permute-start(bf16[32,2304]{1,0:T(8,128)(2,1)S(1)} %get-tuple-element.20), channel_id=1, source_target_pairs={{0,6},{1,7},{2,4},{3,5},{4,2},{5,3},{6,0},{7,1},{8,14},{9,15},{10,... | collective-permute-start | bytes 442376 | tf_op jit(solution)/shard_map/ppermute | solution.py:23
  34.2 6.8 %collective-permute-start.6 = (f32[32,2304]{1,0:T(8,128)S(1)}, f32[32,2304]{1,0:T(8,128)S(1)}, u32[]{:S(2)}, u32[]{:S(2)}) collective-permute-start(f32[32,2304]{1,0:T(8,128)S(1)} %fusion.21), channel_id=1, source_target_pairs={{0,1},{1,0},{2,3},{3,2},{4,5},{5,4},{6,7},{7,6},{8,9},{9,8},{10,11... | collective-permute-start | bytes 884744 | tf_op jit(solution)/shard_map/ppermute | solution.py:23
  41.1 6.8 %collective-permute-start.9 = (bf16[32,2304]{1,0:T(8,128)(2,1)S(1)}, bf16[32,2304]{1,0:T(8,128)(2,1)S(1)}, u32[]{:S(2)}, u32[]{:S(2)}) collective-permute-start(bf16[32,2304]{1,0:T(8,128)(2,1)S(1)} %fusion.22), channel_id=1, source_target_pairs={{0,4},{1,5},{2,6},{3,7},{4,0},{5,1},{6,2},{7,3},{8,12},{9,13},{10,... | collective-permute-start | bytes 442376 | tf_op jit(solution)/shard_map/ppermute | solution.py:23
  42.2 7.2 %collective-permute-start.8 = (bf16[32,2304]{1,0:T(8,128)(2,1)S(1)}, bf16[32,2304]{1,0:T(8,128)(2,1)S(1)}, u32[]{:S(2)}, u32[]{:S(2)}) collective-permute-start(bf16[32,2304]{1,0:T(8,128)(2,1)S(1)} %fusion.22), channel_id=1, source_target_pairs={{0,6},{1,7},{2,4},{3,5},{4,2},{5,3},{6,0},{7,1},{8,14},{9,15},{10,... | collective-permute-start | bytes 442376 | tf_op jit(solution)/shard_map/ppermute | solution.py:23
  43.9 6.7 %collective-permute-start.7 = (bf16[32,2304]{1,0:T(8,128)(2,1)S(1)}, bf16[32,2304]{1,0:T(8,128)(2,1)S(1)}, u32[]{:S(2)}, u32[]{:S(2)}) collective-permute-start(bf16[32,2304]{1,0:T(8,128)(2,1)S(1)} %fusion.22), channel_id=1, source_target_pairs={{0,2},{1,3},{2,0},{3,1},{4,6},{5,7},{6,4},{7,5},{8,10},{9,11},{10,... | collective-permute-start | bytes 442376 | tf_op jit(solution)/shard_map/ppermute | solution.py:23
  50.7 10.0 %collective-permute-start.10 = (bf16[128,2304]{1,0:T(8,128)(2,1)S(1)}, bf16[128,2304]{1,0:T(8,128)(2,1)S(1)}, u32[]{:S(2)}, u32[]{:S(2)}) collective-permute-start(bf16[128,2304]{1,0:T(8,128)(2,1)S(1)} %pad_maximum_fusion.9), channel_id=1, source_target_pairs={{0,8},{1,9},{2,10},{3,11},{4,12},{5,13},{6,14},{7,15},{8,0},{9,1},... | collective-permute-start | bytes 1769480 | tf_op jit(solution)/shard_map/ppermute | solution.py:23
  52.6 17.5 %collective-permute-start.11 = (bf16[128,2304]{1,0:T(8,128)(2,1)S(1)}, bf16[128,2304]{1,0:T(8,128)(2,1)S(1)}, u32[]{:S(2)}, u32[]{:S(2)}) collective-permute-start(bf16[128,2304]{1,0:T(8,128)(2,1)S(1)} %pad_maximum_fusion.9), channel_id=1, source_target_pairs={{0,24},{1,25},{2,26},{3,27},{4,28},{5,29},{6,30},{7,31},{8,16},{9,... | collective-permute-start | bytes 1769480 | tf_op jit(solution)/shard_map/ppermute | solution.py:23
  53.8 16.3 %collective-permute-start.12 = (bf16[128,2304]{1,0:T(8,128)(2,1)S(1)}, bf16[128,2304]{1,0:T(8,128)(2,1)S(1)}, u32[]{:S(2)}, u32[]{:S(2)}) collective-permute-start(bf16[128,2304]{1,0:T(8,128)(2,1)S(1)} %pad_maximum_fusion.9), channel_id=1, source_target_pairs={{0,16},{1,17},{2,18},{3,19},{4,20},{5,21},{6,22},{7,23},{8,24},{9,... | collective-permute-start | bytes 1769480 | tf_op jit(solution)/shard_map/ppermute | solution.py:23
  61.2 10.0 %copy-start.8 = (f32[512]{0:T(512)S(1)}, f32[512]{0:T(512)}, u32[]{:S(2)}) copy-start(f32[512]{0:T(512)} %param.12) | copy-start | bytes 6148
  61.2 10.1 %copy-start.7 = (s32[512]{0:T(512)S(1)}, s32[512]{0:T(512)}, u32[]{:S(2)}) copy-start(s32[512]{0:T(512)} %param.15) | copy-start | bytes 6148
  61.2 10.1 %collective-permute-start.13 = (f32[256,256]{1,0:T(8,128)S(1)}, f32[256,256]{1,0:T(8,128)S(1)}, u32[]{:S(2)}, u32[]{:S(2)}) collective-permute-start(f32[256,256]{1,0:T(8,128)S(1)} %pad_maximum_fusion.14), channel_id=1, source_target_pairs={{0,32},{1,33},{2,34},{3,35},{4,36},{5,37},{6,38},{7,39},{8,40},{9,... | collective-permute-start | bytes 786440 | tf_op jit(solution)/shard_map/ppermute | solution.py:23
  70.9 1.8 collective-permute-start.14
  73.0 8.8 %collective-permute-start.15 = (bf16[128,256]{1,0:T(8,128)(2,1)S(1)}, bf16[128,256]{1,0:T(8,128)(2,1)S(1)}, u32[]{:S(2)}, u32[]{:S(2)}) collective-permute-start(bf16[128,256]{1,0:T(8,128)(2,1)S(1)} %get-tuple-element.31), channel_id=1, source_target_pairs={{0,64},{1,65},{2,66},{3,67},{4,68},{5,69},{6,70},{7,71},{8,72},{9,... | collective-permute-start | bytes 196616 | tf_op jit(solution)/shard_map/ppermute | solution.py:23
  76.4 9.0 %collective-permute-start.17 = (bf16[128,256]{1,0:T(8,128)(2,1)S(1)}, bf16[128,256]{1,0:T(8,128)(2,1)S(1)}, u32[]{:S(2)}, u32[]{:S(2)}) collective-permute-start(bf16[128,256]{1,0:T(8,128)(2,1)S(1)} %get-tuple-element.32), channel_id=1, source_target_pairs={{0,128},{1,129},{2,130},{3,131},{4,132},{5,133},{6,134},{7,135},{8... | collective-permute-start | bytes 196616 | tf_op jit(solution)/shard_map/ppermute | solution.py:23
  81.8 6.4 %collective-permute-start.16 = (bf16[128,256]{1,0:T(8,128)(2,1)S(1)}, bf16[128,256]{1,0:T(8,128)(2,1)S(1)}, u32[]{:S(2)}, u32[]{:S(2)}) collective-permute-start(bf16[128,256]{1,0:T(8,128)(2,1)S(1)} %get-tuple-element.33), channel_id=1, source_target_pairs={{0,192},{1,193},{2,194},{3,195},{4,196},{5,197},{6,198},{7,199},{8... | collective-permute-start | bytes 196616 | tf_op jit(solution)/shard_map/ppermute | solution.py:23
  88.2 9.5 %collective-permute-start.20 = (bf16[128,256]{1,0:T(8,128)(2,1)S(1)}, bf16[128,256]{1,0:T(8,128)(2,1)S(1)}, u32[]{:S(2)}, u32[]{:S(2)}) collective-permute-start(bf16[128,256]{1,0:T(8,128)(2,1)S(1)} %multiply_convert_fusion), channel_id=1, source_target_pairs={{0,128},{1,129},{2,130},{3,131},{4,132},{5,133},{6,134},{7,135},{8... | collective-permute-start | bytes 196616 | tf_op jit(solution)/shard_map/ppermute | solution.py:23
  91.7 6.7 %collective-permute-start.19 = (bf16[128,256]{1,0:T(8,128)(2,1)S(1)}, bf16[128,256]{1,0:T(8,128)(2,1)S(1)}, u32[]{:S(2)}, u32[]{:S(2)}) collective-permute-start(bf16[128,256]{1,0:T(8,128)(2,1)S(1)} %multiply_convert_fusion), channel_id=1, source_target_pairs={{0,192},{1,193},{2,194},{3,195},{4,196},{5,197},{6,198},{7,199},{8... | collective-permute-start | bytes 196616 | tf_op jit(solution)/shard_map/ppermute | solution.py:23
  94.3 5.8 %collective-permute-start.18 = (bf16[128,256]{1,0:T(8,128)(2,1)S(1)}, bf16[128,256]{1,0:T(8,128)(2,1)S(1)}, u32[]{:S(2)}, u32[]{:S(2)}) collective-permute-start(bf16[128,256]{1,0:T(8,128)(2,1)S(1)} %multiply_convert_fusion), channel_id=1, source_target_pairs={{0,64},{1,65},{2,66},{3,67},{4,68},{5,69},{6,70},{7,71},{8,72},{9,... | collective-permute-start | bytes 196616 | tf_op jit(solution)/shard_map/ppermute | solution.py:23
  97.6 2.8 %collective-permute-start.21 = (bf16[128,256]{1,0:T(8,128)(2,1)S(1)}, bf16[128,256]{1,0:T(8,128)(2,1)S(1)}, u32[]{:S(2)}, u32[]{:S(2)}) collective-permute-start(bf16[128,256]{1,0:T(8,128)(2,1)S(1)} %multiply_convert_fusion), channel_id=1, source_target_pairs={{0,32},{1,33},{2,34},{3,35},{4,36},{5,37},{6,38},{7,39},{8,40},{9,... | collective-permute-start | bytes 196616 | tf_op jit(solution)/shard_map/ppermute | solution.py:23
  100.1 1.5 collective-permute-start.22
  100.4 20.9 %copy-start.1 = (bf16[256,2304]{1,0:T(8,128)(2,1)}, bf16[256,2304]{1,0:T(8,128)(2,1)S(1)}, u32[]{:S(2)}) copy-start(bf16[256,2304]{1,0:T(8,128)(2,1)S(1)} %get-tuple-element.12) | copy-start | bytes 3538948
  103.5 11.6 %collective-permute-start.25 = (bf16[128,2304]{1,0:T(8,128)(2,1)S(1)}, bf16[128,2304]{1,0:T(8,128)(2,1)S(1)}, u32[]{:S(2)}, u32[]{:S(2)}) collective-permute-start(bf16[128,2304]{1,0:T(8,128)(2,1)S(1)} %convolution_convert_fusion), channel_id=1, source_target_pairs={{0,16},{1,17},{2,18},{3,19},{4,20},{5,21},{6,22},{7,23},{8,24},{9,... | collective-permute-start | bytes 1769480 | tf_op jit(solution)/shard_map/ppermute | solution.py:23
  104.9 16.3 %collective-permute-start.24 = (bf16[128,2304]{1,0:T(8,128)(2,1)S(1)}, bf16[128,2304]{1,0:T(8,128)(2,1)S(1)}, u32[]{:S(2)}, u32[]{:S(2)}) collective-permute-start(bf16[128,2304]{1,0:T(8,128)(2,1)S(1)} %convolution_convert_fusion.1), channel_id=1, source_target_pairs={{0,24},{1,25},{2,26},{3,27},{4,28},{5,29},{6,30},{7,31},{8,16},{9,... | collective-permute-start | bytes 1769480 | tf_op jit(solution)/shard_map/ppermute | solution.py:23
  107.0 14.2 %collective-permute-start.23 = (bf16[128,2304]{1,0:T(8,128)(2,1)S(1)}, bf16[128,2304]{1,0:T(8,128)(2,1)S(1)}, u32[]{:S(2)}, u32[]{:S(2)}) collective-permute-start(bf16[128,2304]{1,0:T(8,128)(2,1)S(1)} %convolution_convert_fusion.2), channel_id=1, source_target_pairs={{0,8},{1,9},{2,10},{3,11},{4,12},{5,13},{6,14},{7,15},{8,0},{9,1},... | collective-permute-start | bytes 1769480 | tf_op jit(solution)/shard_map/ppermute | solution.py:23
  121.8 9.1 %copy-start.5 = (f32[128,2304]{1,0:T(8,128)}, f32[128,2304]{1,0:T(8,128)S(1)}, u32[]{:S(2)}) copy-start(f32[128,2304]{1,0:T(8,128)S(1)} %get-tuple-element.55) | copy-start | bytes 3538948
  121.9 5.2 %collective-permute-start.26 = (bf16[32,2304]{1,0:T(8,128)(2,1)S(1)}, bf16[32,2304]{1,0:T(8,128)(2,1)S(1)}, u32[]{:S(2)}, u32[]{:S(2)}) collective-permute-start(bf16[32,2304]{1,0:T(8,128)(2,1)S(1)} %get-tuple-element.15), channel_id=1, source_target_pairs={{0,2},{1,3},{2,0},{3,1},{4,6},{5,7},{6,4},{7,5},{8,10},{9,11},{10,... | collective-permute-start | bytes 442376 | tf_op jit(solution)/shard_map/ppermute | solution.py:23
  122.7 6.6 %collective-permute-start.28 = (bf16[32,2304]{1,0:T(8,128)(2,1)S(1)}, bf16[32,2304]{1,0:T(8,128)(2,1)S(1)}, u32[]{:S(2)}, u32[]{:S(2)}) collective-permute-start(bf16[32,2304]{1,0:T(8,128)(2,1)S(1)} %get-tuple-element.16), channel_id=1, source_target_pairs={{0,4},{1,5},{2,6},{3,7},{4,0},{5,1},{6,2},{7,3},{8,12},{9,13},{10,... | collective-permute-start | bytes 442376 | tf_op jit(solution)/shard_map/ppermute | solution.py:23
  124.6 6.4 %collective-permute-start.27 = (bf16[32,2304]{1,0:T(8,128)(2,1)S(1)}, bf16[32,2304]{1,0:T(8,128)(2,1)S(1)}, u32[]{:S(2)}, u32[]{:S(2)}) collective-permute-start(bf16[32,2304]{1,0:T(8,128)(2,1)S(1)} %get-tuple-element.17), channel_id=1, source_target_pairs={{0,6},{1,7},{2,4},{3,5},{4,2},{5,3},{6,0},{7,1},{8,14},{9,15},{10,... | collective-permute-start | bytes 442376 | tf_op jit(solution)/shard_map/ppermute | solution.py:23
  131.0 5.2 %collective-permute-start.29 = (bf16[32,2304]{1,0:T(8,128)(2,1)S(1)}, bf16[32,2304]{1,0:T(8,128)(2,1)S(1)}, u32[]{:S(2)}, u32[]{:S(2)}) collective-permute-start(bf16[32,2304]{1,0:T(8,128)(2,1)S(1)} %fusion.45), channel_id=1, source_target_pairs={{0,1},{1,0},{2,3},{3,2},{4,5},{5,4},{6,7},{7,6},{8,9},{9,8},{10,11... | collective-permute-start | bytes 442376 | tf_op jit(solution)/shard_map/ppermute | solution.py:23
  136.3 15.5 %copy-start.3 = (bf16[256,2304]{1,0:T(8,128)(2,1)S(1)}, bf16[256,2304]{1,0:T(8,128)(2,1)}, u32[]{:S(2)}) copy-start(bf16[256,2304]{1,0:T(8,128)(2,1)} %get-tuple-element.9) | copy-start | bytes 3538948
  136.3 15.5 %copy-start.4 = (bf16[256,2304]{1,0:T(8,128)(2,1)S(1)}, bf16[256,2304]{1,0:T(8,128)(2,1)}, u32[]{:S(2)}) copy-start(bf16[256,2304]{1,0:T(8,128)(2,1)} %get-tuple-element.10) | copy-start | bytes 3538948
  137.5 7.0 %collective-permute-start.32 = (bf16[32,2304]{1,0:T(8,128)(2,1)S(1)}, bf16[32,2304]{1,0:T(8,128)(2,1)S(1)}, u32[]{:S(2)}, u32[]{:S(2)}) collective-permute-start(bf16[32,2304]{1,0:T(8,128)(2,1)S(1)} %get-tuple-element.7), channel_id=1, source_target_pairs={{0,4},{1,5},{2,6},{3,7},{4,0},{5,1},{6,2},{7,3},{8,12},{9,13},{10,... | collective-permute-start | bytes 442376 | tf_op jit(solution)/shard_map/ppermute | solution.py:23
  139.7 6.4 %collective-permute-start.31 = (bf16[32,2304]{1,0:T(8,128)(2,1)S(1)}, bf16[32,2304]{1,0:T(8,128)(2,1)S(1)}, u32[]{:S(2)}, u32[]{:S(2)}) collective-permute-start(bf16[32,2304]{1,0:T(8,128)(2,1)S(1)} %get-tuple-element.7), channel_id=1, source_target_pairs={{0,6},{1,7},{2,4},{3,5},{4,2},{5,3},{6,0},{7,1},{8,14},{9,15},{10,... | collective-permute-start | bytes 442376 | tf_op jit(solution)/shard_map/ppermute | solution.py:23
  140.8 6.2 %collective-permute-start.30 = (bf16[32,2304]{1,0:T(8,128)(2,1)S(1)}, bf16[32,2304]{1,0:T(8,128)(2,1)S(1)}, u32[]{:S(2)}, u32[]{:S(2)}) collective-permute-start(bf16[32,2304]{1,0:T(8,128)(2,1)S(1)} %get-tuple-element.7), channel_id=1, source_target_pairs={{0,2},{1,3},{2,0},{3,1},{4,6},{5,7},{6,4},{7,5},{8,10},{9,11},{10,... | collective-permute-start | bytes 442376 | tf_op jit(solution)/shard_map/ppermute | solution.py:23
  147.0 10.0 %collective-permute-start.33 = (bf16[128,2304]{1,0:T(8,128)(2,1)S(1)}, bf16[128,2304]{1,0:T(8,128)(2,1)S(1)}, u32[]{:S(2)}, u32[]{:S(2)}) collective-permute-start(bf16[128,2304]{1,0:T(8,128)(2,1)S(1)} %pad_maximum_fusion.10), channel_id=1, source_target_pairs={{0,8},{1,9},{2,10},{3,11},{4,12},{5,13},{6,14},{7,15},{8,0},{9,1},... | collective-permute-start | bytes 1769480 | tf_op jit(solution)/shard_map/ppermute | solution.py:23
  148.4 18.6 %collective-permute-start.35 = (bf16[128,2304]{1,0:T(8,128)(2,1)S(1)}, bf16[128,2304]{1,0:T(8,128)(2,1)S(1)}, u32[]{:S(2)}, u32[]{:S(2)}) collective-permute-start(bf16[128,2304]{1,0:T(8,128)(2,1)S(1)} %pad_maximum_fusion.10), channel_id=1, source_target_pairs={{0,16},{1,17},{2,18},{3,19},{4,20},{5,21},{6,22},{7,23},{8,24},{9,... | collective-permute-start | bytes 1769480 | tf_op jit(solution)/shard_map/ppermute | solution.py:23
  149.6 17.4 %collective-permute-start.34 = (bf16[128,2304]{1,0:T(8,128)(2,1)S(1)}, bf16[128,2304]{1,0:T(8,128)(2,1)S(1)}, u32[]{:S(2)}, u32[]{:S(2)}) collective-permute-start(bf16[128,2304]{1,0:T(8,128)(2,1)S(1)} %pad_maximum_fusion.10), channel_id=1, source_target_pairs={{0,24},{1,25},{2,26},{3,27},{4,28},{5,29},{6,30},{7,31},{8,16},{9,... | collective-permute-start | bytes 1769480 | tf_op jit(solution)/shard_map/ppermute | solution.py:23
  158.8 10.0 %collective-permute-start.36 = (f32[256,256]{1,0:T(8,128)S(1)}, f32[256,256]{1,0:T(8,128)S(1)}, u32[]{:S(2)}, u32[]{:S(2)}) collective-permute-start(f32[256,256]{1,0:T(8,128)S(1)} %pad_maximum_fusion.15), channel_id=1, source_target_pairs={{0,32},{1,33},{2,34},{3,35},{4,36},{5,37},{6,38},{7,39},{8,40},{9,... | collective-permute-start | bytes 786440 | tf_op jit(solution)/shard_map/ppermute | solution.py:23
  168.8 1.6 collective-permute-start.37
  170.7 7.2 %collective-permute-start.38 = (bf16[128,256]{1,0:T(8,128)(2,1)S(1)}, bf16[128,256]{1,0:T(8,128)(2,1)S(1)}, u32[]{:S(2)}, u32[]{:S(2)}) collective-permute-start(bf16[128,256]{1,0:T(8,128)(2,1)S(1)} %get-tuple-element.21), channel_id=1, source_target_pairs={{0,64},{1,65},{2,66},{3,67},{4,68},{5,69},{6,70},{7,71},{8,72},{9,... | collective-permute-start | bytes 196616 | tf_op jit(solution)/shard_map/ppermute | solution.py:23
  171.8 8.3 %collective-permute-start.40 = (bf16[128,256]{1,0:T(8,128)(2,1)S(1)}, bf16[128,256]{1,0:T(8,128)(2,1)S(1)}, u32[]{:S(2)}, u32[]{:S(2)}) collective-permute-start(bf16[128,256]{1,0:T(8,128)(2,1)S(1)} %get-tuple-element.22), channel_id=1, source_target_pairs={{0,128},{1,129},{2,130},{3,131},{4,132},{5,133},{6,134},{7,135},{8... | collective-permute-start | bytes 196616 | tf_op jit(solution)/shard_map/ppermute | solution.py:23
  176.0 7.1 %collective-permute-start.39 = (bf16[128,256]{1,0:T(8,128)(2,1)S(1)}, bf16[128,256]{1,0:T(8,128)(2,1)S(1)}, u32[]{:S(2)}, u32[]{:S(2)}) collective-permute-start(bf16[128,256]{1,0:T(8,128)(2,1)S(1)} %get-tuple-element.23), channel_id=1, source_target_pairs={{0,192},{1,193},{2,194},{3,195},{4,196},{5,197},{6,198},{7,199},{8... | collective-permute-start | bytes 196616 | tf_op jit(solution)/shard_map/ppermute | solution.py:23
  183.2 1.3 collective-permute-start.41
  (3 other events, 5.4 us)
